TPU v7x, 512 devices: a whole 4x4x16 slice. The times are simulated.
512 devices in a mesh: patch: 32 (over z, core), line: 16 (over y, x).
Axes of the slice: x: 4, y: 4, z: 16, core: 2. Of those that a mesh axis runs over, the one named last changes fastest.
Arguments:
- residual: float32 [128, 80, 2, 4096], P('line', None, None, 'patch'), may hold values from -6 to 6
- forward_maps: float32 [32, 128, 6400], P('patch', 'line'), as said below
- pivot_inverse: float32 [32, 128, 6400], P('patch', 'line'), as said below
- backward_maps: float32 [32, 128, 6400], P('patch', 'line'), as said below
- face_flux: float32 [32, 128, 4, 6400], P('patch', 'line'), as said below
- mass_scale: float32 [128, 4096], P('line', 'patch'), may hold values from 0.2 to 1
- frequencies: float32 [2], replicated, may hold values from 0.25 to 1
- line_order: int32 [4096], P('patch'), may hold values from 0 to 127, as said below
Outputs:
- update: float32 [128, 80, 2, 4096], P('line', None, None, 'patch')
- next_residual: float32 [128, 80, 2, 4096], P('line', None, None, 'patch')
Inputs may be any that keep to these rules, and one draw needn't show every extreme that they name: `line_order`: for each patch, its 128 entries are a permutation of 0 to 127. `forward_maps`: each block, read row by row, is the real form [[a, -b], [b, a]] of a complex block a + i b. `pivot_inverse`: each block, read row by row, is the real form [[a, -b], [b, a]] of a complex block a + i b. `backward_maps`: each block, read row by row, is the real form [[a, -b], [b, a]] of a complex block a + i b. `face_flux`: each block, read row by row, is the real form [[a, -b], [b, a]] of a complex block a + i b.
All inputs are finite; a program needn't handle non-finite values.
Results may differ from a plain program's by a relative error of at most 0.00012.
Values sent between devices are 32-bit elements; how exact they have to be, the bound alone decides.
A program may use at most 64 MiB of HBM per device.

v0:
```python
import functools

import jax
import jax.numpy as jnp
from jax import lax
from jax.experimental import pallas as pl
from jax.experimental.pallas import tpu as pltpu
from jax.sharding import PartitionSpec as P

SX = 32
RELAXATION = 0.8
KEEP = 1.0 - RELAXATION
C = 40
W = 80
K = 8
L = 128
SIDE = 4
F32 = jnp.float32
BF16 = jnp.bfloat16
MESH = pl.DeviceIdType.MESH


def lanes(rows, width=L):
    return lax.broadcasted_iota(jnp.int32, (rows, width), 1)


def roll(x, by):
    by = by % L
    return x if by == 0 else pltpu.roll(x, by, 1)


def two(x):
    high = x.astype(BF16)
    return high, (x - high.astype(F32)).astype(BF16)


def rhs_of(x):
    high, low = two(x)
    return jnp.concatenate([high, low, high, jnp.zeros((16, x.shape[1]), BF16)], axis=0)


def lhs_of(w):
    lane = lanes(w.shape[0])
    high = w.astype(BF16).astype(F32)
    low = w - high
    moved = roll(high, W)
    first = jnp.where(lane < W, high, moved)
    second = jnp.where(lane < 32, moved, roll(low, 32))
    return jnp.concatenate([first, second], axis=1).astype(BF16)


def real_form(tile, at):
    lane = lanes(W)
    plain = roll(tile, -at)
    moved = roll(tile, C - at)
    turned = jnp.concatenate([-moved[C:], moved[:C]], axis=0)
    return jnp.where(lane < C, plain, jnp.where(lane < W, turned, 0.0))


def whole_map(top):
    lane = lanes(C)
    top = jnp.where(lane < W, top, 0.0)
    bottom = jnp.where(lane < C, -roll(top, -C), jnp.where(lane < W, roll(top, C), 0.0))
    return jnp.concatenate([top, bottom], axis=0)


def mm(a, b):
    return jnp.dot(a, b, preferred_element_type=F32)


def band(x, lo, hi):
    lane = lanes(x.shape[0])
    return jnp.where((lane >= lo) & (lane < hi), x, 0.0)


def eye_at(at):
    row = lax.broadcasted_iota(jnp.int32, (W, L), 0)
    return jnp.where(lanes(W) == row + at, jnp.where(row < C, 1.0, 0.0), 0.0)


def unfold(load, store, rows):
    lane = lanes(rows)
    for group in range(5):
        parts = [load(5 * group + q) for q in range(5)]
        for r in range(8):
            q, off = divmod(W * r, L)
            piece = roll(parts[q], -off)
            if off + W > L:
                piece = jnp.where(lane < L - off, piece, roll(parts[q + 1], -off))
            store(8 * group + r, piece)


def kernel(
    res, fwd, piv, bwd, flux, mass, freq, order,
    upd_out, res_out,
    tops, xtops, fd, bn, fx, qh, rp, dp, cp,
    st, zz, yl, ym, upd, ph, heads,
    sx, rx, sxm, rxm, sy, ry, sym, rym, sz, rz, ww, cw,
    sl, sh, hl, hh,
    send_x, recv_x, send_xm, recv_xm, send_y, recv_y, send_ym, recv_ym,
    send_z, recv_z, send_l, recv_l, send_h, recv_h,
):
    patch = lax.axis_index("patch")
    line = lax.axis_index("line")
    patches = lax.axis_size("patch")
    my_y, my_x = line // SIDE, line % SIDE
    before = lax.rem(patch + patches - 1, patches)
    after = lax.rem(patch + 1, patches)

    def in_row(d):
        return lax.rem(my_x + d, SIDE)

    def in_column(d):
        return lax.rem(my_y + d, SIDE)

    def row_peer(d):
        return (patch, my_y * SIDE + in_row(d))

    def column_peer(d):
        return (patch, in_column(d) * SIDE + my_x)

    barrier = pltpu.get_barrier_semaphore()
    for d in range(1, SIDE):
        pl.semaphore_signal(barrier, inc=1, device_id=row_peer(d), device_id_type=MESH)
        pl.semaphore_signal(barrier, inc=1, device_id=column_peer(d), device_id_type=MESH)
    pl.semaphore_signal(barrier, inc=1, device_id=(before, line), device_id_type=MESH)
    pl.semaphore_signal(barrier, inc=1, device_id=(after, line), device_id_type=MESH)

    started = []

    def send(src, dst, out_sem, in_sem, to):
        copy = pltpu.make_async_remote_copy(
            src_ref=src, dst_ref=dst, send_sem=out_sem, recv_sem=in_sem,
            device_id=to, device_id_type=MESH,
        )
        copy.start()
        started.append(copy)
        return copy

    lane = lanes(W)

    place = lax.broadcasted_iota(jnp.int32, (L, L), 0)
    hot = jnp.where(order[...] == place, 1.0, 0.0).astype(BF16)
    to_cells = jnp.concatenate([hot, hot], axis=1)
    to_lines = jnp.concatenate([hot, hot], axis=0)

    def pair(x):
        return jnp.concatenate(two(x), axis=1)

    def grid(x):
        return lax.dot_general(
            pair(x), to_cells, (((1,), (1,)), ((), ())), preferred_element_type=F32
        )

    def stored(x):
        return mm(pair(x), to_lines)

    def unfold_map(ref, which):
        def load(q):
            return ref[0, :, L * q : L * (q + 1)]

        def store(i, piece):
            tops[which, pl.ds(i, K, stride=C), :] = piece

        unfold(load, store, K)

    for which, ref in enumerate((fwd, piv, bwd)):
        unfold_map(ref, which)

    def prepare(k, carry):
        at = pl.ds(k * C, C)
        fd[k, 0:W, :] = lhs_of(whole_map(tops[0, at, :]))
        fd[k + 1, W : 2 * W, :] = lhs_of(whole_map(tops[1, at, :]))
        bn[k] = lhs_of(-whole_map(tops[2, at, :]))
        for f in range(2):
            st[k, :, L * f : L * (f + 1)] = grid(res[k, pl.ds(f, W, stride=2), :])
        return carry

    lax.fori_loop(0, K, prepare, 0)

    cells_mass = grid(mass[...])
    for f in range(2):
        ph[:, L * f : L * (f + 1)] = freq[f] * cells_mass

    pl.semaphore_wait(barrier, 8)

    def unfold_flux(k, carry):
        def load(q):
            return flux[0, k, :, L * q : L * (q + 1)]

        def store(i, piece):
            xtops[pl.ds(i, 4, stride=C), :] = piece

        unfold(load, store, 4)
        for d in range(4):
            fx[k, d] = lhs_of(whole_map(xtops[d * C : (d + 1) * C, :]))
        return carry

    def pack_back(k, carry):
        tile = ym[k]
        at = pl.ds(pl.multiple_of(k * W, W), W)
        qh[at, 0:256] = lhs_of(real_form(tile, 80))
        qh[at, 256:512] = lhs_of(real_form(tile, 40))
        return carry

    def local_chain(first):
        width = 384 if first else 256
        x = st[0]
        if first:
            top = whole_map(tops[0, 0:C, :])
            x = jnp.concatenate([x, band(roll(top, 80), 80, 120)], axis=1)

        def down(k, x):
            r = mm(fd[k], rhs_of(x))
            zz[k - 1, :, 0:width] = r[W:]
            new = r[:W, 0:256] + st[k]
            if first:
                new = jnp.concatenate([new, r[:W, 256:]], axis=1)
            return new

        x = lax.fori_loop(1, K, down, x)
        heads[0] = x[:, 0:L]
        heads[1] = x[:, L : 2 * L]
        end = mm(fd[K, W : 2 * W, :], rhs_of(x))
        if first:
            back = -whole_map(tops[2, (K - 1) * C : K * C, :])
            end_map = end[:, 256:] + band(roll(back, 40), 40, 80)
            ym[K - 1] = end_map
            end = jnp.concatenate([end[:, :256], end_map], axis=1)
        yl[K - 1] = end[:, :256]

        def climb(step, y):
            k = K - 2 - step
            y = mm(bn[k], rhs_of(y)) + zz[k, :, 0:width]
            yl[k] = y[:, :256]
            if first:
                ym[k] = y[:, 256:]
            return y

        y = lax.fori_loop(0, K - 1, climb, end)
        if first:
            return roll(x[:, 256:], 48) + y[:, 256:]
        return None

    def pack_maps(ref, j, tile):
        ref[j, 0:W, :] = lhs_of(real_form(tile, 0))
        ref[j, W : 2 * W, :] = lhs_of(real_form(tile, 80))
        ref[j, 2 * W : 3 * W, :] = lhs_of(real_form(tile, 40))

    def row_solve(s, first):
        v = [rx[s, j] for j in range(SIDE)]
        join = (lambda a, b: jnp.concatenate([a, b], axis=1)) if first else (lambda a, b: a)
        w = [None, v[0]]
        q = [None]
        if first:
            m = [rxm[j] for j in range(SIDE)]
            wm = [eye_at(80), band(roll(m[0], 80), 80, 120)]
            qm = [band(m[0], 80, 120)]
        for j in range(1, SIDE):
            r = mm(rp[j, 0 : 2 * W, :], rhs_of(join(w[j], wm[j] if first else None)))
            w.append(r[:W, :L] + v[j])
            q.append(r[W:, :L])
            if first:
                wm.append(r[:W, L:])
                qm.append(r[W:, L:])
        y = [None] * SIDE
        cur = v[3] + roll(q[3], 64)
        if first:
            y_map = [None] * SIDE
            y_map[3] = eye_at(40)
            cur_map = band(m[3], 40, 80) + qm[3]
        for j in (2, 1, 0):
            y[j] = cur
            if first:
                y_map[j] = cur_map
            r = mm(rp[j, 2 * W :, :], rhs_of(join(cur, cur_map if first else None)))
            cur = r[:, :L] + v[j]
            if j:
                cur = cur + roll(q[j], 64)
            if first:
                cur_map = r[:, L:] + qm[j]
        half = lane < 64
        for j in range(SIDE):
            lo = w[j] if j else 0.0
            hi = y[j] if j < 3 else 0.0
            ww[j] = jnp.where(half, lo, hi)
        sy[s] = jnp.where(half, w[4], cur)
        if first:
            sym[...] = roll(wm[4], 48) + cur_map
            for j in range(SIDE):
                cw[j] = wm[j] + jnp.where(lane < 80, y_map[j], 0.0)
                cw[j + 4] = band(y_map[j], 80, 120)

    def pack_row(j, carry):
        tile = cw[j]
        dp[j, 0:W, :] = lhs_of(real_form(tile, 80))
        dp[j, W : 2 * W, :] = lhs_of(real_form(tile, 40))
        dp[j, 2 * W :, :] = lhs_of(real_form(cw[j + 4], 80))
        return carry

    def column_solve(s):
        v = [ry[s, j] for j in range(SIDE)]
        w = [None, v[0]]
        q = [None]
        for j in (1, 2):
            r = mm(cp[j, 0 : 2 * W, :], rhs_of(w[j]))
            w.append(r[:W] + v[j])
            q.append(r[W:])
        q.append(mm(cp[3, W : 2 * W, :], rhs_of(w[3])))
        y = [None] * SIDE
        cur = v[3] + roll(q[3], 64)
        for j in (2, 1):
            y[j] = cur
            cur = mm(cp[j, 2 * W :, :], rhs_of(cur)) + v[j] + roll(q[j], 64)
        y[0] = cur
        half = lane < 64
        for j in range(SIDE):
            cw[8 + j] = jnp.where(half, w[j] if j else 0.0, y[j] if j < 3 else 0.0)
        return cw[8 + my_y]

    def edges(m):
        low = high = None
        for i in range(4):
            tile = yl[2 * m + i // 2, :, L * (i % 2) : L * (i % 2 + 1)]
            a, b = roll(tile, 32 * i), roll(tile, 32 * (i + 1))
            low = a if i == 0 else jnp.where(lane >= 32 * i, a, low)
            high = b if i == 0 else jnp.where(lane >= 32 * i, b, high)
        return low, high

    column = lax.rem(lane, SX)

    for s in range(2):
        first = s == 0
        maps = local_chain(first)
        half = lane < 64
        for f in range(2):
            t, u = heads[f], yl[0, :, L * f : L * (f + 1)]
            sx[s, 2 * f] = jnp.where(half, t, roll(u, 64))
            sx[s, 2 * f + 1] = jnp.where(half, roll(t, 64), u)
        copies = []
        if first:
            sxm[...] = maps
        for d in (2, 1, 3):
            copies.append(
                send(sx.at[s, in_row(d)], rx.at[s, my_x], send_x.at[s, d], recv_x.at[s, d], row_peer(d))
            )
            if first:
                copies.append(send(sxm, rxm.at[my_x], send_xm.at[d], recv_xm.at[d], row_peer(d)))
        rx[s, my_x] = sx[s, my_x]
        if first:
            rxm[my_x] = maps
            lax.fori_loop(0, K, pack_back, 0)
        for copy in copies:
            copy.wait_recv()
        if first:
            for j in range(SIDE):
                pack_maps(rp, j, rxm[j])
        row_solve(s, first)

        copies = []
        for d in (2, 1, 3):
            copies.append(send(sy.at[s], ry.at[s, my_y], send_y.at[s, d], recv_y.at[s, d], column_peer(d)))
            if first:
                copies.append(send(sym, rym.at[my_y], send_ym.at[d], recv_ym.at[d], column_peer(d)))
        ry[s, my_y] = sy[s]
        if first:
            rym[my_y] = sym[...]
            lax.fori_loop(0, SIDE, pack_row, 0)
            lax.fori_loop(0, K, unfold_flux, 0)
        for copy in copies:
            copy.wait_recv()
        if first:
            for j in range(SIDE):
                pack_maps(cp, j, rym[j])
        entry = rhs_of(column_solve(s))

        for j in range(SIDE):
            r = mm(dp[j], entry)
            sz[s, j] = ww[j] + jnp.where(half, r[:W], r[W : 2 * W] + roll(r[2 * W :], 64))
        copies = []
        for d in (2, 1, 3):
            copies.append(
                send(sz.at[s, in_row(d)], rz.at[s, my_x], send_z.at[s, d], recv_z.at[s, d], row_peer(d))
            )
        rz[s, my_x] = sz[s, my_x]
        for copy in copies:
            copy.wait_recv()
        z = [rz[s, j] for j in range(SIDE)]
        incoming = jnp.concatenate(
            [jnp.where(half, z[2 * f], roll(z[2 * f + 1], 64)) for f in range(2)], axis=1
        )
        arriving = jnp.concatenate(
            [jnp.where(half, roll(z[2 * f], 64), z[2 * f + 1]) for f in range(2)], axis=1
        )
        both = jnp.concatenate([rhs_of(incoming), rhs_of(arriving)], axis=0)

        low_copies, high_copies = [], []
        for m in range(4):
            r = mm(qh[2 * W * m : 2 * W * (m + 1), :], both)
            for i in range(2):
                k = 2 * m + i
                y = yl[k] + r[W * i : W * (i + 1)]
                yl[k] = y
                upd[k] = RELAXATION * y if first else upd[k] + RELAXATION * y
            low, high = edges(m)
            sl[s, m] = low
            sh[s, m] = high
            high_copies.append(send(sl.at[s, m], hh.at[s, m], send_l.at[s, m], recv_l.at[s, m], (before, line)))
            low_copies.append(send(sh.at[s, m], hl.at[s, m], send_h.at[s, m], recv_h.at[s, m], (after, line)))

        def inner(k, carry):
            y = yl[k]
            ups, downs = [], []
            for f in range(2):
                tile = y[:, L * f : L * (f + 1)]
                ups.append(jnp.where(column > 0, roll(tile, 1), 0.0))
                downs.append(jnp.where(column < SX - 1, roll(tile, -1), 0.0))
            acc = mm(fx[k, 0], rhs_of(jnp.concatenate(ups, axis=1)))
            acc = acc + mm(fx[k, 1], rhs_of(jnp.concatenate(downs, axis=1)))
            turned = jnp.concatenate([-y[C:], y[:C]], axis=0)
            acc = acc + ph[pl.ds(k, 1), :] * turned
            st[k] = KEEP * st[k] - RELAXATION * acc
            if not first:
                for f in range(2):
                    upd_out[k, pl.ds(f, W, stride=2), :] = stored(upd[k, :, L * f : L * (f + 1)])
            return carry

        lax.fori_loop(0, K, inner, 0)

        for m in range(4):
            low_copies[m].wait_recv()
            high_copies[m].wait_recv()
            for i in range(2):
                k = 2 * m + i
                lows, highs = [], []
                for f in range(2):
                    tile = yl[k, :, L * f : L * (f + 1)]
                    slot = 32 * (2 * i + f)
                    lows.append(jnp.where(lane < SX, roll(hl[s, m], -slot), roll(tile, SX)))
                    highs.append(jnp.where(lane >= L - SX, roll(hh[s, m], 96 - slot), roll(tile, -SX)))
                acc = mm(fx[k, 2], rhs_of(jnp.concatenate(lows, axis=1)))
                acc = acc + mm(fx[k, 3], rhs_of(jnp.concatenate(highs, axis=1)))
                current = st[k] - RELAXATION * acc
                if first:
                    st[k] = current
                else:
                    for f in range(2):
                        res_out[k, pl.ds(f, W, stride=2), :] = stored(current[:, L * f : L * (f + 1)])

    for copy in started:
        copy.wait_send()


def shards(residual, forward_maps, pivot_inverse, backward_maps, face_flux, mass_scale, frequencies, line_order):
    vmem = pl.BlockSpec(memory_space=pltpu.VMEM)
    smem = pl.BlockSpec(memory_space=pltpu.SMEM)
    dma = pltpu.SemaphoreType.DMA
    out = jax.ShapeDtypeStruct((K, 2 * W, L), F32)
    update, left = pl.pallas_call(
        kernel,
        out_shape=(out, out),
        in_specs=[vmem, vmem, vmem, vmem, vmem, vmem, smem, vmem],
        out_specs=(vmem, vmem),
        scratch_shapes=[
            pltpu.VMEM((3, K * C, L), F32),
            pltpu.VMEM((4 * C, L), F32),
            pltpu.VMEM((K + 1, 2 * W, 256), BF16),
            pltpu.VMEM((K, W, 256), BF16),
            pltpu.VMEM((K, 4, W, 256), BF16),
            pltpu.VMEM((K * W, 512), BF16),
            pltpu.VMEM((SIDE, 3 * W, 256), BF16),
            pltpu.VMEM((SIDE, 3 * W, 256), BF16),
            pltpu.VMEM((SIDE, 3 * W, 256), BF16),
            pltpu.VMEM((K, W, 256), F32),
            pltpu.VMEM((K, W, 384), F32),
            pltpu.VMEM((K, W, 256), F32),
            pltpu.VMEM((K, W, L), F32),
            pltpu.VMEM((K, W, 256), F32),
            pltpu.VMEM((K, 256), F32),
            pltpu.VMEM((2, W, L), F32),
            pltpu.VMEM((2, SIDE, W, L), F32),
            pltpu.VMEM((2, SIDE, W, L), F32),
            pltpu.VMEM((W, L), F32),
            pltpu.VMEM((SIDE, W, L), F32),
            pltpu.VMEM((2, W, L), F32),
            pltpu.VMEM((2, SIDE, W, L), F32),
            pltpu.VMEM((W, L), F32),
            pltpu.VMEM((SIDE, W, L), F32),
            pltpu.VMEM((2, SIDE, W, L), F32),
            pltpu.VMEM((2, SIDE, W, L), F32),
            pltpu.VMEM((SIDE, W, L), F32),
            pltpu.VMEM((3 * SIDE, W, L), F32),
            pltpu.VMEM((2, 4, W, L), F32),
            pltpu.VMEM((2, 4, W, L), F32),
            pltpu.VMEM((2, 4, W, L), F32),
            pltpu.VMEM((2, 4, W, L), F32),
            dma((2, SIDE)), dma((2, SIDE)), dma((SIDE,)), dma((SIDE,)),
            dma((2, SIDE)), dma((2, SIDE)), dma((SIDE,)), dma((SIDE,)),
            dma((2, SIDE)), dma((2, SIDE)),
            dma((2, 4)), dma((2, 4)), dma((2, 4)), dma((2, 4)),
        ],
        compiler_params=pltpu.CompilerParams(collective_id=0, has_side_effects=True),
        name="sweeps",
    )(
        residual.reshape(K, 2 * W, L), forward_maps, pivot_inverse, backward_maps, face_flux,
        mass_scale, frequencies, line_order.reshape(1, L),
    )
    return update.reshape(K, W, 2, L), left.reshape(K, W, 2, L)


def solution(mesh):
    maps = P("patch", "line", None)
    state = P("line", None, None, "patch")
    placed = (state, maps, maps, maps, P("patch", "line", None, None), P("line", "patch"), P(), P("patch"))
    return jax.shard_map(
        shards, mesh=mesh, in_specs=placed, out_specs=(state, state), check_vma=False
    )
```

profile of v0, /device:TPU:8, one launch (start us, length us, event | category | flops | bytes accessed | tf_op | source)
XLA Modules:
  0.0 67.0 jit_solution(16715145461335317498)
XLA Ops:
  0.6 63.5 %sweeps.1 = (f32[8,160,128]{2,1,0:T(8,128)}, f32[8,160,128]{2,1,0:T(8,128)}) custom-call(f32[8,160,128]{2,1,0:T(8,128)} %bitcast.6, f32[1,8,6400]{2,1,0:T(8,128)} %fwd.1, f32[1,8,6400]{2,1,0:T(8,128)} %piv.1, f32[1,8,6400]{2,1,0:T(8,128)} %bwd.1, f32[1,8,4,6400]{3,2,1,0:T(4,128)} %flux.1, f32[8,128]{1,0:T(8,128)} %mass.1, f32[2]{0:T(128)} %freq.1, ...), custom_call_target="tpu_custom_call" | custom-call | tf_op jit(solution)/shard_map/sweeps/pallas_call | solution.py:459
  64.1 0.0 copy-start
  64.2 2.0 %copy.12 = f32[8,80,2,128]{3,2,1,0:T(2,128)} copy(f32[8,80,2,128]{3,2,1,0:T(2,128)} %bitcast.5) | data formatting | bytes 1310720
  66.2 0.0 copy-done
  66.2 0.8 %copy.13 = f32[8,80,2,128]{3,2,1,0:T(2,128)} copy(f32[8,80,2,128]{3,2,1,0:T(2,128)S(1)} %bitcast.4) | data formatting | bytes 1310720
Async XLA Ops:
  64.1 2.0 %copy-start = (f32[8,160,128]{2,1,0:T(8,128)S(1)}, f32[8,160,128]{2,1,0:T(8,128)}, u32[]{:S(2)}) copy-start(f32[8,160,128]{2,1,0:T(8,128)} %get-tuple-element.5) | copy-start | bytes 1966084
where the time goes:
time: 67.2 us; the launch traced here: 67 us
  Pallas kernels  63.5 us (94%)
  local copies, waits for them, and re-layouts  2.88 us (4%)
    pallas_call x1, Pallas kernels, shards(): pl.pallas_call(kernel, out_shape=(out, out), in_specs=[vmem, vmem, vmem,...  63.5 us
    unnamed x4, local copies, waits for them, and re-layouts  2.88 us

commit v1 on v0

--- a/solution.py
+++ b/solution.py
@@ -91,10 +91,11 @@
 
 
 def kernel(
-    res, fwd, piv, bwd, flux, mass, freq, order,
+    res_in, fwd_in, piv_in, bwd_in, flux_in, mass_in, freq_in, order_in,
     upd_out, res_out,
+    res, fwd, piv, bwd, flux, mass, freq, order, load_sem,
     tops, xtops, fd, bn, fx, qh, rp, dp, cp,
-    st, zz, yl, ym, upd, ph, heads,
+    st, zz, yl, ym, upd, ph,
     sx, rx, sxm, rxm, sy, ry, sym, rym, sz, rz, ww, cw,
     sl, sh, hl, hh,
     send_x, recv_x, send_xm, recv_xm, send_y, recv_y, send_ym, recv_ym,
@@ -126,6 +127,23 @@
     pl.semaphore_signal(barrier, inc=1, device_id=(before, line), device_id_type=MESH)
     pl.semaphore_signal(barrier, inc=1, device_id=(after, line), device_id_type=MESH)
 
+    half_map = C * W
+    loads = [
+        pltpu.make_async_copy(a, b, load_sem.at[i])
+        for i, (a, b) in enumerate((
+            (fwd_in.at[0, :, 0:half_map], fwd),
+            (order_in, order),
+            (res_in, res),
+            (piv_in.at[0, :, 0:half_map], piv),
+            (bwd_in.at[0, :, 0:half_map], bwd),
+            (mass_in, mass),
+            (freq_in, freq),
+            (flux_in.at[0, :, :, 0:half_map], flux),
+        ))
+    ]
+    for copy in loads:
+        copy.start()
+
     started = []
 
     def send(src, dst, out_sem, in_sem, to):
@@ -139,6 +157,19 @@
 
     lane = lanes(W)
 
+    def unfold_map(ref, which):
+        def load(q):
+            return ref[:, L * q : L * (q + 1)]
+
+        def store(i, piece):
+            tops[which, pl.ds(i, K, stride=C), :] = piece
+
+        unfold(load, store, K)
+
+    loads[0].wait()
+    unfold_map(fwd, 0)
+    loads[1].wait()
+
     place = lax.broadcasted_iota(jnp.int32, (L, L), 0)
     hot = jnp.where(order[...] == place, 1.0, 0.0).astype(BF16)
     to_cells = jnp.concatenate([hot, hot], axis=1)
@@ -155,45 +186,36 @@
     def stored(x):
         return mm(pair(x), to_lines)
 
-    def unfold_map(ref, which):
-        def load(q):
-            return ref[0, :, L * q : L * (q + 1)]
-
-        def store(i, piece):
-            tops[which, pl.ds(i, K, stride=C), :] = piece
-
-        unfold(load, store, K)
-
-    for which, ref in enumerate((fwd, piv, bwd)):
-        unfold_map(ref, which)
-
-    def prepare(k, carry):
-        at = pl.ds(k * C, C)
-        fd[k, 0:W, :] = lhs_of(whole_map(tops[0, at, :]))
-        fd[k + 1, W : 2 * W, :] = lhs_of(whole_map(tops[1, at, :]))
-        bn[k] = lhs_of(-whole_map(tops[2, at, :]))
-        for f in range(2):
-            st[k, :, L * f : L * (f + 1)] = grid(res[k, pl.ds(f, W, stride=2), :])
-        return carry
-
-    lax.fori_loop(0, K, prepare, 0)
-
-    cells_mass = grid(mass[...])
+    def top_of(which, k):
+        return whole_map(tops[which, k * C : (k + 1) * C, :])
+
+    def pack_down(k):
+        if k < K:
+            fd[k, 0:W, :] = lhs_of(top_of(0, k))
+            for f in range(2):
+                st[k, :, L * f : L * (f + 1)] = grid(res[k, pl.ds(f, W, stride=2), :])
+        fd[k, W : 2 * W, :] = lhs_of(top_of(1, k - 1))
+        bn[k - 1] = lhs_of(-top_of(2, k - 1))
+
+    loads[2].wait()
+    loads[3].wait()
+    unfold_map(piv, 1)
+    loads[4].wait()
+    unfold_map(bwd, 2)
     for f in range(2):
-        ph[:, L * f : L * (f + 1)] = freq[f] * cells_mass
-
-    pl.semaphore_wait(barrier, 8)
+        st[0, :, L * f : L * (f + 1)] = grid(res[0, pl.ds(f, W, stride=2), :])
+    pack_down(1)
 
     def unfold_flux(k, carry):
         def load(q):
-            return flux[0, k, :, L * q : L * (q + 1)]
+            return flux[k, :, L * q : L * (q + 1)]
 
         def store(i, piece):
             xtops[pl.ds(i, 4, stride=C), :] = piece
 
         unfold(load, store, 4)
         for d in range(4):
-            fx[k, d] = lhs_of(whole_map(xtops[d * C : (d + 1) * C, :]))
+            fx[k, d * W : (d + 1) * W, :] = lhs_of(whole_map(xtops[d * C : (d + 1) * C, :]))
         return carry
 
     def pack_back(k, carry):
@@ -203,44 +225,31 @@
         qh[at, 256:512] = lhs_of(real_form(tile, 40))
         return carry
 
-    def local_chain(first):
-        width = 384 if first else 256
-        x = st[0]
-        if first:
-            top = whole_map(tops[0, 0:C, :])
-            x = jnp.concatenate([x, band(roll(top, 80), 80, 120)], axis=1)
-
-        def down(k, x):
-            r = mm(fd[k], rhs_of(x))
-            zz[k - 1, :, 0:width] = r[W:]
-            new = r[:W, 0:256] + st[k]
-            if first:
-                new = jnp.concatenate([new, r[:W, 256:]], axis=1)
-            return new
-
-        x = lax.fori_loop(1, K, down, x)
-        heads[0] = x[:, 0:L]
-        heads[1] = x[:, L : 2 * L]
+    def step_down(k, x):
+        r = mm(fd[k], rhs_of(x))
+        zz[k - 1, :, 0 : x.shape[1]] = r[W:]
+        new = r[:W, 0:256] + st[k]
+        if x.shape[1] > 256:
+            new = jnp.concatenate([new, r[:W, 256:]], axis=1)
+        return new
+
+    def local_back(x):
+        first = x.shape[1] > 256
         end = mm(fd[K, W : 2 * W, :], rhs_of(x))
         if first:
-            back = -whole_map(tops[2, (K - 1) * C : K * C, :])
-            end_map = end[:, 256:] + band(roll(back, 40), 40, 80)
+            end_map = end[:, 256:] + band(roll(-top_of(2, K - 1), 40), 40, 80)
             ym[K - 1] = end_map
             end = jnp.concatenate([end[:, :256], end_map], axis=1)
         yl[K - 1] = end[:, :256]
-
-        def climb(step, y):
-            k = K - 2 - step
-            y = mm(bn[k], rhs_of(y)) + zz[k, :, 0:width]
+        y = end
+        for k in range(K - 2, -1, -1):
+            y = mm(bn[k], rhs_of(y)) + zz[k, :, 0 : x.shape[1]]
             yl[k] = y[:, :256]
             if first:
                 ym[k] = y[:, 256:]
-            return y
-
-        y = lax.fori_loop(0, K - 1, climb, end)
-        if first:
-            return roll(x[:, 256:], 48) + y[:, 256:]
-        return None
+        if first:
+            return y, roll(x[:, 256:], 48) + y[:, 256:]
+        return y, None
 
     def pack_maps(ref, j, tile):
         ref[j, 0:W, :] = lhs_of(real_form(tile, 0))
@@ -331,10 +340,16 @@
 
     for s in range(2):
         first = s == 0
-        maps = local_chain(first)
+        if first:
+            x = jnp.concatenate([st[0], band(roll(top_of(0, 0), 80), 80, 120)], axis=1)
+            for k in range(1, K):
+                pack_down(k + 1)
+                x = step_down(k, x)
+            pl.semaphore_wait(barrier, 8)
+        y, maps = local_back(x)
         half = lane < 64
         for f in range(2):
-            t, u = heads[f], yl[0, :, L * f : L * (f + 1)]
+            t, u = x[:, L * f : L * (f + 1)], y[:, L * f : L * (f + 1)]
             sx[s, 2 * f] = jnp.where(half, t, roll(u, 64))
             sx[s, 2 * f + 1] = jnp.where(half, roll(t, 64), u)
         copies = []
@@ -350,6 +365,11 @@
         if first:
             rxm[my_x] = maps
             lax.fori_loop(0, K, pack_back, 0)
+            loads[5].wait()
+            loads[6].wait()
+            cells_mass = grid(mass[...])
+            for f in range(2):
+                ph[:, L * f : L * (f + 1)] = freq[f] * cells_mass
         for copy in copies:
             copy.wait_recv()
         if first:
@@ -366,6 +386,7 @@
         if first:
             rym[my_y] = sym[...]
             lax.fori_loop(0, SIDE, pack_row, 0)
+            loads[7].wait()
             lax.fori_loop(0, K, unfold_flux, 0)
         for copy in copies:
             copy.wait_recv()
@@ -410,15 +431,17 @@
 
         def inner(k, carry):
             y = yl[k]
-            ups, downs = [], []
+            r = mm(fx[k], rhs_of(y))
+            parts = []
             for f in range(2):
-                tile = y[:, L * f : L * (f + 1)]
-                ups.append(jnp.where(column > 0, roll(tile, 1), 0.0))
-                downs.append(jnp.where(column < SX - 1, roll(tile, -1), 0.0))
-            acc = mm(fx[k, 0], rhs_of(jnp.concatenate(ups, axis=1)))
-            acc = acc + mm(fx[k, 1], rhs_of(jnp.concatenate(downs, axis=1)))
+                at = slice(L * f, L * (f + 1))
+                acc = jnp.where(column > 0, roll(r[0:W, at], 1), 0.0)
+                acc = acc + jnp.where(column < SX - 1, roll(r[W : 2 * W, at], -1), 0.0)
+                acc = acc + jnp.where(lane >= SX, roll(r[2 * W : 3 * W, at], SX), 0.0)
+                acc = acc + jnp.where(lane < L - SX, roll(r[3 * W :, at], -SX), 0.0)
+                parts.append(acc)
             turned = jnp.concatenate([-y[C:], y[:C]], axis=0)
-            acc = acc + ph[pl.ds(k, 1), :] * turned
+            acc = jnp.concatenate(parts, axis=1) + ph[pl.ds(k, 1), :] * turned
             st[k] = KEEP * st[k] - RELAXATION * acc
             if not first:
                 for f in range(2):
@@ -430,19 +453,21 @@
         for m in range(4):
             low_copies[m].wait_recv()
             high_copies[m].wait_recv()
+            k0, k1 = 2 * m, 2 * m + 1
+            r_low = mm(jnp.concatenate([fx[k0, 2 * W : 3 * W, :], fx[k1, 2 * W : 3 * W, :]], axis=0), rhs_of(hl[s, m]))
+            r_high = mm(jnp.concatenate([fx[k0, 3 * W :, :], fx[k1, 3 * W :, :]], axis=0), rhs_of(hh[s, m]))
             for i in range(2):
                 k = 2 * m + i
-                lows, highs = [], []
+                parts = []
                 for f in range(2):
-                    tile = yl[k, :, L * f : L * (f + 1)]
                     slot = 32 * (2 * i + f)
-                    lows.append(jnp.where(lane < SX, roll(hl[s, m], -slot), roll(tile, SX)))
-                    highs.append(jnp.where(lane >= L - SX, roll(hh[s, m], 96 - slot), roll(tile, -SX)))
-                acc = mm(fx[k, 2], rhs_of(jnp.concatenate(lows, axis=1)))
-                acc = acc + mm(fx[k, 3], rhs_of(jnp.concatenate(highs, axis=1)))
-                current = st[k] - RELAXATION * acc
+                    low = roll(r_low[W * i : W * (i + 1)], -slot)
+                    high = roll(r_high[W * i : W * (i + 1)], 96 - slot)
+                    parts.append(jnp.where(lane < SX, low, jnp.where(lane >= L - SX, high, 0.0)))
+                current = st[k] - RELAXATION * jnp.concatenate(parts, axis=1)
                 if first:
                     st[k] = current
+                    x = step_down(k, x) if k else current
                 else:
                     for f in range(2):
                         res_out[k, pl.ds(f, W, stride=2), :] = stored(current[:, L * f : L * (f + 1)])
@@ -453,20 +478,29 @@
 
 def shards(residual, forward_maps, pivot_inverse, backward_maps, face_flux, mass_scale, frequencies, line_order):
     vmem = pl.BlockSpec(memory_space=pltpu.VMEM)
-    smem = pl.BlockSpec(memory_space=pltpu.SMEM)
+    anywhere = pl.BlockSpec(memory_space=pl.ANY)
     dma = pltpu.SemaphoreType.DMA
-    out = jax.ShapeDtypeStruct((K, 2 * W, L), F32)
+    out = pltpu.VMEM((K, 2 * W, L), F32)
     update, left = pl.pallas_call(
         kernel,
         out_shape=(out, out),
-        in_specs=[vmem, vmem, vmem, vmem, vmem, vmem, smem, vmem],
+        in_specs=[anywhere] * 8,
         out_specs=(vmem, vmem),
         scratch_shapes=[
+            pltpu.VMEM((K, 2 * W, L), F32),
+            pltpu.VMEM((K, C * W), F32),
+            pltpu.VMEM((K, C * W), F32),
+            pltpu.VMEM((K, C * W), F32),
+            pltpu.VMEM((K, 4, C * W), F32),
+            pltpu.VMEM((K, L), F32),
+            pltpu.SMEM((2,), F32),
+            pltpu.VMEM((1, L), jnp.int32),
+            dma((8,)),
             pltpu.VMEM((3, K * C, L), F32),
             pltpu.VMEM((4 * C, L), F32),
             pltpu.VMEM((K + 1, 2 * W, 256), BF16),
             pltpu.VMEM((K, W, 256), BF16),
-            pltpu.VMEM((K, 4, W, 256), BF16),
+            pltpu.VMEM((K, 4 * W, 256), BF16),
             pltpu.VMEM((K * W, 512), BF16),
             pltpu.VMEM((SIDE, 3 * W, 256), BF16),
             pltpu.VMEM((SIDE, 3 * W, 256), BF16),
@@ -477,7 +511,6 @@
             pltpu.VMEM((K, W, L), F32),
             pltpu.VMEM((K, W, 256), F32),
             pltpu.VMEM((K, 256), F32),
-            pltpu.VMEM((2, W, L), F32),
             pltpu.VMEM((2, SIDE, W, L), F32),
             pltpu.VMEM((2, SIDE, W, L), F32),
             pltpu.VMEM((W, L), F32),

time: 67.2 us -> 61.2 us (0.911)
  Pallas kernels: 63.5 us -> 58.7 us
  local copies, waits for them, and re-layouts: 2.88 us -> 1.67 us
    pallas_call x1, Pallas kernels: 63.5 us -> 58.7 us  [shards(): pl.pallas_call(kernel, out_shape=(out, out), in_specs=[anywhere] * 8, out...]
    unnamed x4 -> x2, local copies, waits for them, and re-layouts: 2.88 us -> 1.67 us
where the time goes in v1:
time: 61.2 us; the launch traced here: 61.1 us
  Pallas kernels  58.7 us (96%)
  local copies, waits for them, and re-layouts  1.67 us (3%)
  between operations  0.64 us (1%)
    pallas_call x1, Pallas kernels, shards(): pl.pallas_call(kernel, out_shape=(out, out), in_specs=[anywhere] * 8, out...  58.7 us
    unnamed x2, local copies, waits for them, and re-layouts  1.67 us

profile of v1, /device:TPU:8, one launch (start us, length us, event | category | flops | bytes accessed | tf_op | source)
XLA Modules:
  0.0 61.1 jit_solution(15628735483072768833)
XLA Ops:
  0.6 58.7 %sweeps.1 = (f32[8,160,128]{2,1,0:T(8,128)S(1)}, f32[8,160,128]{2,1,0:T(8,128)S(1)}) custom-call(f32[8,160,128]{2,1,0:T(8,128)} %bitcast.6, f32[1,8,6400]{2,1,0:T(8,128)} %fwd_in.1, f32[1,8,6400]{2,1,0:T(8,128)} %piv_in.1, f32[1,8,6400]{2,1,0:T(8,128)} %bwd_in.1, f32[1,8,4,6400]{3,2,1,0:T(4,128)} %flux_in.1, f32[8,128]{1,0:T(8,128)} %mass_in.1, f32[2]{0:T(128)} %freq_in.1, ...), custom_call_target="tpu_custom_call" | custom-call | tf_op jit(solution)/shard_map/sweeps/pallas_call | solution.py:484
  59.4 0.8 %copy.12 = f32[8,80,2,128]{3,2,1,0:T(2,128)} copy(f32[8,80,2,128]{3,2,1,0:T(2,128)S(1)} %bitcast.5) | data formatting | bytes 1310720
  60.2 0.8 %copy.13 = f32[8,80,2,128]{3,2,1,0:T(2,128)} copy(f32[8,80,2,128]{3,2,1,0:T(2,128)S(1)} %bitcast.4) | data formatting | bytes 1310720

commit v2 on v1

--- a/solution.py
+++ b/solution.py
@@ -96,10 +96,10 @@
     res, fwd, piv, bwd, flux, mass, freq, order, load_sem,
     tops, xtops, fd, bn, fx, qh, rp, dp, cp,
     st, zz, yl, ym, upd, ph,
-    sx, rx, sxm, rxm, sy, ry, sym, rym, sz, rz, ww, cw,
+    stx, rtx, sux, rux, sty, rty, suy, ruy, swz, rwz, syz, ryz, yloc, cw, pick,
     sl, sh, hl, hh,
-    send_x, recv_x, send_xm, recv_xm, send_y, recv_y, send_ym, recv_ym,
-    send_z, recv_z, send_l, recv_l, send_h, recv_h,
+    out_tx, in_tx, out_ux, in_ux, out_ty, in_ty, out_uy, in_uy,
+    out_wz, in_wz, out_yz, in_yz, send_l, recv_l, send_h, recv_h,
 ):
     patch = lax.axis_index("patch")
     line = lax.axis_index("line")
@@ -221,8 +221,8 @@
     def pack_back(k, carry):
         tile = ym[k]
         at = pl.ds(pl.multiple_of(k * W, W), W)
-        qh[at, 0:256] = lhs_of(real_form(tile, 80))
-        qh[at, 256:512] = lhs_of(real_form(tile, 40))
+        qh[0, at, :] = lhs_of(real_form(tile, 80))
+        qh[1, at, :] = lhs_of(real_form(tile, 40))
         return carry
 
     def step_down(k, x):
@@ -251,81 +251,39 @@
             return y, roll(x[:, 256:], 48) + y[:, 256:]
         return y, None
 
-    def pack_maps(ref, j, tile):
-        ref[j, 0:W, :] = lhs_of(real_form(tile, 0))
-        ref[j, W : 2 * W, :] = lhs_of(real_form(tile, 80))
-        ref[j, 2 * W : 3 * W, :] = lhs_of(real_form(tile, 40))
-
-    def row_solve(s, first):
-        v = [rx[s, j] for j in range(SIDE)]
-        join = (lambda a, b: jnp.concatenate([a, b], axis=1)) if first else (lambda a, b: a)
-        w = [None, v[0]]
-        q = [None]
-        if first:
-            m = [rxm[j] for j in range(SIDE)]
-            wm = [eye_at(80), band(roll(m[0], 80), 80, 120)]
-            qm = [band(m[0], 80, 120)]
-        for j in range(1, SIDE):
-            r = mm(rp[j, 0 : 2 * W, :], rhs_of(join(w[j], wm[j] if first else None)))
-            w.append(r[:W, :L] + v[j])
-            q.append(r[W:, :L])
-            if first:
-                wm.append(r[:W, L:])
-                qm.append(r[W:, L:])
-        y = [None] * SIDE
-        cur = v[3] + roll(q[3], 64)
-        if first:
-            y_map = [None] * SIDE
-            y_map[3] = eye_at(40)
-            cur_map = band(m[3], 40, 80) + qm[3]
-        for j in (2, 1, 0):
-            y[j] = cur
-            if first:
-                y_map[j] = cur_map
-            r = mm(rp[j, 2 * W :, :], rhs_of(join(cur, cur_map if first else None)))
-            cur = r[:, :L] + v[j]
-            if j:
-                cur = cur + roll(q[j], 64)
-            if first:
-                cur_map = r[:, L:] + qm[j]
-        half = lane < 64
-        for j in range(SIDE):
-            lo = w[j] if j else 0.0
-            hi = y[j] if j < 3 else 0.0
-            ww[j] = jnp.where(half, lo, hi)
-        sy[s] = jnp.where(half, w[4], cur)
-        if first:
-            sym[...] = roll(wm[4], 48) + cur_map
-            for j in range(SIDE):
-                cw[j] = wm[j] + jnp.where(lane < 80, y_map[j], 0.0)
-                cw[j + 4] = band(y_map[j], 80, 120)
+    def fold_low(x):
+        return jnp.where(lanes(C) < 64, x[:C], roll(x[C:], 64))
+
+    def fold_high(x):
+        return jnp.where(lanes(C) < 64, roll(x[:C], 64), x[C:])
+
+    def unfold_low(x):
+        return jnp.concatenate([x, roll(x, 64)], axis=0)
+
+    def join(x, extra):
+        return x if extra is None else jnp.concatenate([x, extra], axis=1)
 
     def pack_row(j, carry):
+        at = pl.ds(pl.multiple_of(j * W, W), W)
         tile = cw[j]
-        dp[j, 0:W, :] = lhs_of(real_form(tile, 80))
-        dp[j, W : 2 * W, :] = lhs_of(real_form(tile, 40))
-        dp[j, 2 * W :, :] = lhs_of(real_form(cw[j + 4], 80))
+        dp[0, at, :] = lhs_of(real_form(tile, 80))
+        dp[1, at, :] = lhs_of(real_form(cw[j + SIDE], 80))
+        dp[2, at, :] = lhs_of(real_form(tile, 40))
         return carry
 
-    def column_solve(s):
-        v = [ry[s, j] for j in range(SIDE)]
-        w = [None, v[0]]
-        q = [None]
-        for j in (1, 2):
-            r = mm(cp[j, 0 : 2 * W, :], rhs_of(w[j]))
-            w.append(r[:W] + v[j])
-            q.append(r[W:])
-        q.append(mm(cp[3, W : 2 * W, :], rhs_of(w[3])))
-        y = [None] * SIDE
-        cur = v[3] + roll(q[3], 64)
-        for j in (2, 1):
-            y[j] = cur
-            cur = mm(cp[j, 2 * W :, :], rhs_of(cur)) + v[j] + roll(q[j], 64)
-        y[0] = cur
-        half = lane < 64
-        for j in range(SIDE):
-            cw[8 + j] = jnp.where(half, w[j] if j else 0.0, y[j] if j < 3 else 0.0)
-        return cw[8 + my_y]
+    def to_row(src, dst, out_sem, in_sem):
+        copies = [send(src(in_row(d)), dst(my_x), out_sem.at[d], in_sem.at[d], row_peer(d)) for d in (2, 1, 3)]
+        dst(my_x)[...] = src(my_x)[...]
+        return copies
+
+    def to_column(src, dst, out_sem, in_sem):
+        copies = [send(src, dst(my_y), out_sem.at[d], in_sem.at[d], column_peer(d)) for d in (2, 1, 3)]
+        dst(my_y)[...] = src[...]
+        return copies
+
+    def arrived(copies):
+        for copy in copies:
+            copy.wait_recv()
 
     def edges(m):
         low = high = None
@@ -346,78 +304,175 @@
                 pack_down(k + 1)
                 x = step_down(k, x)
             pl.semaphore_wait(barrier, 8)
+        for f in range(2):
+            t = x[:, L * f : L * (f + 1)]
+            stx[s, 2 * f, 0:C, :] = fold_low(t)
+            stx[s, 2 * f + 1, 0:C, :] = fold_high(t)
+        if first:
+            fold = fold_low(roll(x[:, 256:], 48))
+            for j in range(SIDE):
+                stx[s, j, C:W, :] = fold
+        rows = W if first else C
+        t_copies = to_row(
+            lambda j: stx.at[s, j, 0:rows], lambda j: rtx.at[s, j, 0:rows], out_tx.at[s], in_tx.at[s]
+        )
+
         y, maps = local_back(x)
-        half = lane < 64
         for f in range(2):
-            t, u = x[:, L * f : L * (f + 1)], y[:, L * f : L * (f + 1)]
-            sx[s, 2 * f] = jnp.where(half, t, roll(u, 64))
-            sx[s, 2 * f + 1] = jnp.where(half, roll(t, 64), u)
-        copies = []
-        if first:
-            sxm[...] = maps
-        for d in (2, 1, 3):
-            copies.append(
-                send(sx.at[s, in_row(d)], rx.at[s, my_x], send_x.at[s, d], recv_x.at[s, d], row_peer(d))
-            )
-            if first:
-                copies.append(send(sxm, rxm.at[my_x], send_xm.at[d], recv_xm.at[d], row_peer(d)))
-        rx[s, my_x] = sx[s, my_x]
-        if first:
-            rxm[my_x] = maps
+            u = y[:, L * f : L * (f + 1)]
+            sux[s, 2 * f, 0:C, :] = fold_low(u)
+            sux[s, 2 * f + 1, 0:C, :] = fold_high(u)
+        if first:
+            for j in range(SIDE):
+                sux[s, j, C:, :] = maps
+        back_rows = W + C if first else C
+        u_copies = to_row(
+            lambda j: sux.at[s, j, 0:back_rows], lambda j: rux.at[s, j, 0:back_rows], out_ux.at[s], in_ux.at[s]
+        )
+        if first:
             lax.fori_loop(0, K, pack_back, 0)
             loads[5].wait()
             loads[6].wait()
             cells_mass = grid(mass[...])
             for f in range(2):
                 ph[:, L * f : L * (f + 1)] = freq[f] * cells_mass
-        for copy in copies:
-            copy.wait_recv()
+
+        arrived(t_copies)
+        t = [unfold_low(rtx[s, j, 0:C, :]) for j in range(SIDE)]
+        w, wm, w_rhs, q, qm = [None, t[0]], [None] * 5, [None], [None], [None] * SIDE
+        if first:
+            m = [unfold_low(rtx[s, j, C:W, :]) for j in range(SIDE)]
+            for j in range(1, SIDE):
+                rp[j, 0:W, :] = lhs_of(real_form(m[j], 0))
+            wm[0:2] = [eye_at(80), band(roll(m[0], 80), 80, 120)]
+        for j in range(1, SIDE):
+            w_rhs.append(rhs_of(join(w[j], wm[j])))
+            r = mm(rp[j, 0 : W if first else 2 * W, :], w_rhs[j])
+            w.append(r[:W, :L] + t[j])
+            if first:
+                wm[j + 1] = r[:, L:]
+            else:
+                q.append(r[W:])
+        sty[s, 0:C, :] = fold_low(w[4])
+        if first:
+            sty[s, C:W, :] = fold_low(roll(wm[4], 48))
+        t_copies = to_column(
+            sty.at[s, 0:rows], lambda j: rty.at[s, j, 0:rows], out_ty.at[s], in_ty.at[s]
+        )
+
+        arrived(u_copies)
+        u = [unfold_low(rux[s, j, 0:C, :]) for j in range(SIDE)]
+        v, vm = [None] * SIDE, [None] * SIDE
+        cur_map = None
+        if first:
+            nq = [rux[s, j, C:, :] for j in range(SIDE)]
+            qm[0] = band(nq[0], 80, 120)
+            for j in range(1, SIDE):
+                rp[j, W : 2 * W, :] = lhs_of(real_form(nq[j], 80))
+                r = mm(rp[j, W : 2 * W, :], w_rhs[j])
+                q.append(r[:, :L])
+                qm[j] = r[:, L:]
+            for j in range(SIDE - 1):
+                rp[j, 2 * W :, :] = lhs_of(real_form(nq[j], 40))
+            vm[3] = eye_at(40)
+            cur_map = band(nq[3], 40, 80) + qm[3]
+        cur = u[3] + q[3]
+        for j in (2, 1, 0):
+            v[j], vm[j] = cur, cur_map
+            r = mm(rp[j, 2 * W :, :], rhs_of(join(cur, cur_map)))
+            cur = r[:, :L] + u[j]
+            if j:
+                cur = cur + q[j]
+            if first:
+                cur_map = r[:, L:] + qm[j]
+        suy[s, 0:C, :] = fold_low(cur)
+        if first:
+            suy[s, C:, :] = cur_map
+        u_copies = to_column(
+            suy.at[s, 0:back_rows], lambda j: ruy.at[s, j, 0:back_rows], out_uy.at[s], in_uy.at[s]
+        )
         if first:
             for j in range(SIDE):
-                pack_maps(rp, j, rxm[j])
-        row_solve(s, first)
-
-        copies = []
-        for d in (2, 1, 3):
-            copies.append(send(sy.at[s], ry.at[s, my_y], send_y.at[s, d], recv_y.at[s, d], column_peer(d)))
-            if first:
-                copies.append(send(sym, rym.at[my_y], send_ym.at[d], recv_ym.at[d], column_peer(d)))
-        ry[s, my_y] = sy[s]
-        if first:
-            rym[my_y] = sym[...]
+                cw[j] = wm[j] + band(vm[j], 40, 80)
+                cw[j + SIDE] = vm[j]
             lax.fori_loop(0, SIDE, pack_row, 0)
             loads[7].wait()
-            lax.fori_loop(0, K, unfold_flux, 0)
-        for copy in copies:
-            copy.wait_recv()
-        if first:
-            for j in range(SIDE):
-                pack_maps(cp, j, rym[j])
-        entry = rhs_of(column_solve(s))
-
+            lax.fori_loop(0, K // 2, unfold_flux, 0)
+        w_own, v_own = w, v
+
+        arrived(t_copies)
+        t = [unfold_low(rty[s, j, 0:C, :]) for j in range(SIDE)]
+        if first:
+            for j in (1, 2):
+                cp[j, 0:W, :] = lhs_of(real_form(unfold_low(rty[s, j, C:W, :]), 0))
+        w, w_rhs, q = [jnp.zeros((W, L), F32), t[0]], [None], [None]
+        for j in (1, 2):
+            w_rhs.append(rhs_of(w[j]))
+            r = mm(cp[j, 0 : W if first else 2 * W, :], w_rhs[j])
+            w.append(r[:W] + t[j])
+            if not first:
+                q.append(r[W:])
+        w_rhs.append(rhs_of(w[3]))
         for j in range(SIDE):
-            r = mm(dp[j], entry)
-            sz[s, j] = ww[j] + jnp.where(half, r[:W], r[W : 2 * W] + roll(r[2 * W :], 64))
-        copies = []
-        for d in (2, 1, 3):
-            copies.append(
-                send(sz.at[s, in_row(d)], rz.at[s, my_x], send_z.at[s, d], recv_z.at[s, d], row_peer(d))
-            )
-        rz[s, my_x] = sz[s, my_x]
-        for copy in copies:
-            copy.wait_recv()
-        z = [rz[s, j] for j in range(SIDE)]
-        incoming = jnp.concatenate(
-            [jnp.where(half, z[2 * f], roll(z[2 * f + 1], 64)) for f in range(2)], axis=1
-        )
-        arriving = jnp.concatenate(
-            [jnp.where(half, roll(z[2 * f], 64), z[2 * f + 1]) for f in range(2)], axis=1
-        )
-        both = jnp.concatenate([rhs_of(incoming), rhs_of(arriving)], axis=0)
+            pick[j] = w[j]
+        entry = rhs_of(pick[my_y])
+        r = mm(dp[0], entry)
+        for j in range(SIDE):
+            into = r[W * j : W * (j + 1)]
+            swz[s, j] = fold_low(into + w_own[j] if j else into)
+        t_copies = to_row(lambda j: swz.at[s, j], lambda j: rwz.at[s, j], out_wz.at[s], in_wz.at[s])
+        r = mm(dp[1], entry)
+        for j in range(SIDE):
+            into = r[W * j : W * (j + 1)]
+            yloc[j] = into + v_own[j] if j < 3 else into
+        if not first:
+            q.append(mm(cp[3, W : 2 * W, :], w_rhs[3]))
+
+        arrived(u_copies)
+        u = [unfold_low(ruy[s, j, 0:C, :]) for j in range(SIDE)]
+        if first:
+            nq = [ruy[s, j, C:, :] for j in range(SIDE)]
+            for j in range(1, SIDE):
+                cp[j, W : 2 * W, :] = lhs_of(real_form(nq[j], 80))
+                q.append(mm(cp[j, W : 2 * W, :], w_rhs[j]))
+            for j in (1, 2):
+                cp[j, 2 * W :, :] = lhs_of(real_form(nq[j], 40))
+        pick[3] = jnp.zeros((W, L), F32)
+        cur = u[3] + q[3]
+        for j in (2, 1):
+            pick[j] = cur
+            cur = mm(cp[j, 2 * W :, :], rhs_of(cur)) + u[j] + q[j]
+        pick[0] = cur
+        r = mm(dp[2], rhs_of(pick[my_y]))
+        for j in range(SIDE):
+            syz[s, j] = fold_low(r[W * j : W * (j + 1)] + yloc[j])
+        u_copies = to_row(lambda j: syz.at[s, j], lambda j: ryz.at[s, j], out_yz.at[s], in_yz.at[s])
+        if first:
+            lax.fori_loop(K // 2, K, unfold_flux, 0)
+
+        def assemble(ref):
+            tiles = []
+            for f in range(2):
+                a, b = ref[s, 2 * f], ref[s, 2 * f + 1]
+                tiles.append(
+                    jnp.concatenate(
+                        [jnp.where(lanes(C) < 64, a, roll(b, 64)), jnp.where(lanes(C) < 64, roll(a, 64), b)], axis=0
+                    )
+                )
+            return jnp.concatenate(tiles, axis=1)
+
+        arrived(t_copies)
+        incoming = rhs_of(assemble(rwz))
+        for m in range(4):
+            r = mm(qh[0, 2 * W * m : 2 * W * (m + 1), :], incoming)
+            for i in range(2):
+                yl[2 * m + i] = yl[2 * m + i] + r[W * i : W * (i + 1)]
+        arrived(u_copies)
+        arriving = rhs_of(assemble(ryz))
 
         low_copies, high_copies = [], []
         for m in range(4):
-            r = mm(qh[2 * W * m : 2 * W * (m + 1), :], both)
+            r = mm(qh[1, 2 * W * m : 2 * W * (m + 1), :], arriving)
             for i in range(2):
                 k = 2 * m + i
                 y = yl[k] + r[W * i : W * (i + 1)]
@@ -501,9 +556,9 @@
             pltpu.VMEM((K + 1, 2 * W, 256), BF16),
             pltpu.VMEM((K, W, 256), BF16),
             pltpu.VMEM((K, 4 * W, 256), BF16),
-            pltpu.VMEM((K * W, 512), BF16),
+            pltpu.VMEM((2, K * W, 256), BF16),
             pltpu.VMEM((SIDE, 3 * W, 256), BF16),
-            pltpu.VMEM((SIDE, 3 * W, 256), BF16),
+            pltpu.VMEM((3, SIDE * W, 256), BF16),
             pltpu.VMEM((SIDE, 3 * W, 256), BF16),
             pltpu.VMEM((K, W, 256), F32),
             pltpu.VMEM((K, W, 384), F32),
@@ -511,25 +566,19 @@
             pltpu.VMEM((K, W, L), F32),
             pltpu.VMEM((K, W, 256), F32),
             pltpu.VMEM((K, 256), F32),
-            pltpu.VMEM((2, SIDE, W, L), F32),
-            pltpu.VMEM((2, SIDE, W, L), F32),
-            pltpu.VMEM((W, L), F32),
+            pltpu.VMEM((2, SIDE, W, L), F32), pltpu.VMEM((2, SIDE, W, L), F32),
+            pltpu.VMEM((2, SIDE, W + C, L), F32), pltpu.VMEM((2, SIDE, W + C, L), F32),
+            pltpu.VMEM((2, W, L), F32), pltpu.VMEM((2, SIDE, W, L), F32),
+            pltpu.VMEM((2, W + C, L), F32), pltpu.VMEM((2, SIDE, W + C, L), F32),
+            pltpu.VMEM((2, SIDE, C, L), F32), pltpu.VMEM((2, SIDE, C, L), F32),
+            pltpu.VMEM((2, SIDE, C, L), F32), pltpu.VMEM((2, SIDE, C, L), F32),
             pltpu.VMEM((SIDE, W, L), F32),
-            pltpu.VMEM((2, W, L), F32),
-            pltpu.VMEM((2, SIDE, W, L), F32),
-            pltpu.VMEM((W, L), F32),
-            pltpu.VMEM((SIDE, W, L), F32),
-            pltpu.VMEM((2, SIDE, W, L), F32),
-            pltpu.VMEM((2, SIDE, W, L), F32),
-            pltpu.VMEM((SIDE, W, L), F32),
-            pltpu.VMEM((3 * SIDE, W, L), F32),
+            pltpu.VMEM((2 * SIDE, W, L), F32), pltpu.VMEM((SIDE, W, L), F32),
             pltpu.VMEM((2, 4, W, L), F32),
             pltpu.VMEM((2, 4, W, L), F32),
             pltpu.VMEM((2, 4, W, L), F32),
             pltpu.VMEM((2, 4, W, L), F32),
-            dma((2, SIDE)), dma((2, SIDE)), dma((SIDE,)), dma((SIDE,)),
-            dma((2, SIDE)), dma((2, SIDE)), dma((SIDE,)), dma((SIDE,)),
-            dma((2, SIDE)), dma((2, SIDE)),
+            *[dma((2, SIDE)) for _ in range(12)],
             dma((2, 4)), dma((2, 4)), dma((2, 4)), dma((2, 4)),
         ],
         compiler_params=pltpu.CompilerParams(collective_id=0, has_side_effects=True),

time: 61.2 us -> 57 us (0.931)
  Pallas kernels: 58.7 us -> 54.6 us
    pallas_call x1, Pallas kernels: 58.7 us -> 54.6 us  [shards(): pl.pallas_call(kernel, out_shape=(out, out), in_specs=[anywhere] * 8, out...]
where the time goes in v2:
time: 57 us; the launch traced here: 56.9 us
  Pallas kernels  54.6 us (96%)
  local copies, waits for them, and re-layouts  1.67 us (3%)
  between operations  0.64 us (1%)
    pallas_call x1, Pallas kernels, shards(): pl.pallas_call(kernel, out_shape=(out, out), in_specs=[anywhere] * 8, out...  54.6 us
    unnamed x2, local copies, waits for them, and re-layouts  1.67 us

profile of v2, /device:TPU:8, one launch (start us, length us, event | category | flops | bytes accessed | tf_op | source)
XLA Modules:
  0.0 56.9 jit_solution(17738773740111170131)
XLA Ops:
  0.6 54.6 %sweeps.1 = (f32[8,160,128]{2,1,0:T(8,128)S(1)}, f32[8,160,128]{2,1,0:T(8,128)S(1)}) custom-call(f32[8,160,128]{2,1,0:T(8,128)} %bitcast.6, f32[1,8,6400]{2,1,0:T(8,128)} %fwd_in.1, f32[1,8,6400]{2,1,0:T(8,128)} %piv_in.1, f32[1,8,6400]{2,1,0:T(8,128)} %bwd_in.1, f32[1,8,4,6400]{3,2,1,0:T(4,128)} %flux_in.1, f32[8,128]{1,0:T(8,128)} %mass_in.1, f32[2]{0:T(128)} %freq_in.1, ...), custom_call_target="tpu_custom_call" | custom-call | tf_op jit(solution)/shard_map/sweeps/pallas_call | solution.py:539
  55.2 0.8 %copy.12 = f32[8,80,2,128]{3,2,1,0:T(2,128)} copy(f32[8,80,2,128]{3,2,1,0:T(2,128)S(1)} %bitcast.5) | data formatting | bytes 1310720
  56.1 0.8 %copy.13 = f32[8,80,2,128]{3,2,1,0:T(2,128)} copy(f32[8,80,2,128]{3,2,1,0:T(2,128)S(1)} %bitcast.4) | data formatting | bytes 1310720

commit v3 on v2

--- a/solution.py
+++ b/solution.py
@@ -144,7 +144,7 @@
     for copy in loads:
         copy.start()
 
-    started = []
+    sent = []
 
     def send(src, dst, out_sem, in_sem, to):
         copy = pltpu.make_async_remote_copy(
@@ -152,7 +152,6 @@
             device_id=to, device_id_type=MESH,
         )
         copy.start()
-        started.append(copy)
         return copy
 
     lane = lanes(W)
@@ -189,11 +188,14 @@
     def top_of(which, k):
         return whole_map(tops[which, k * C : (k + 1) * C, :])
 
+    def to_grid(k):
+        r = grid(jnp.concatenate([res[k, pl.ds(f, W, stride=2), :] for f in range(2)], axis=0))
+        st[k] = jnp.concatenate([r[:W], r[W:]], axis=1)
+
     def pack_down(k):
         if k < K:
             fd[k, 0:W, :] = lhs_of(top_of(0, k))
-            for f in range(2):
-                st[k, :, L * f : L * (f + 1)] = grid(res[k, pl.ds(f, W, stride=2), :])
+            to_grid(k)
         fd[k, W : 2 * W, :] = lhs_of(top_of(1, k - 1))
         bn[k - 1] = lhs_of(-top_of(2, k - 1))
 
@@ -202,8 +204,7 @@
     unfold_map(piv, 1)
     loads[4].wait()
     unfold_map(bwd, 2)
-    for f in range(2):
-        st[0, :, L * f : L * (f + 1)] = grid(res[0, pl.ds(f, W, stride=2), :])
+    to_grid(0)
     pack_down(1)
 
     def unfold_flux(k, carry):
@@ -271,24 +272,29 @@
         dp[2, at, :] = lhs_of(real_form(tile, 40))
         return carry
 
-    def to_row(src, dst, out_sem, in_sem):
-        copies = [send(src(in_row(d)), dst(my_x), out_sem.at[d], in_sem.at[d], row_peer(d)) for d in (2, 1, 3)]
+    def to_row(src, dst, three, out_sem, in_sem):
+        for d in (2, 1, 3):
+            send(src(in_row(d)), dst(my_x), out_sem, in_sem, row_peer(d))
         dst(my_x)[...] = src(my_x)[...]
-        return copies
-
-    def to_column(src, dst, out_sem, in_sem):
-        copies = [send(src, dst(my_y), out_sem.at[d], in_sem.at[d], column_peer(d)) for d in (2, 1, 3)]
+        sent.append((three, out_sem))
+        return three, in_sem
+
+    def to_column(src, dst, three, out_sem, in_sem):
+        for d in (2, 1, 3):
+            send(src, dst(my_y), out_sem, in_sem, column_peer(d))
         dst(my_y)[...] = src[...]
-        return copies
+        sent.append((three, out_sem))
+        return three, in_sem
+
+    def bytes_of(ref, sem):
+        pltpu.make_async_copy(ref, ref, sem).wait()
 
     def arrived(copies):
-        for copy in copies:
-            copy.wait_recv()
-
-    def edges(m):
+        bytes_of(*copies)
+
+    def edges(pieces):
         low = high = None
-        for i in range(4):
-            tile = yl[2 * m + i // 2, :, L * (i % 2) : L * (i % 2 + 1)]
+        for i, tile in enumerate(pieces):
             a, b = roll(tile, 32 * i), roll(tile, 32 * (i + 1))
             low = a if i == 0 else jnp.where(lane >= 32 * i, a, low)
             high = b if i == 0 else jnp.where(lane >= 32 * i, b, high)
@@ -314,7 +320,8 @@
                 stx[s, j, C:W, :] = fold
         rows = W if first else C
         t_copies = to_row(
-            lambda j: stx.at[s, j, 0:rows], lambda j: rtx.at[s, j, 0:rows], out_tx.at[s], in_tx.at[s]
+            lambda j: stx.at[s, j, 0:rows], lambda j: rtx.at[s, j, 0:rows],
+            rtx.at[s, 0:3, 0:rows], out_tx.at[s], in_tx.at[s]
         )
 
         y, maps = local_back(x)
@@ -327,7 +334,8 @@
                 sux[s, j, C:, :] = maps
         back_rows = W + C if first else C
         u_copies = to_row(
-            lambda j: sux.at[s, j, 0:back_rows], lambda j: rux.at[s, j, 0:back_rows], out_ux.at[s], in_ux.at[s]
+            lambda j: sux.at[s, j, 0:back_rows], lambda j: rux.at[s, j, 0:back_rows],
+            rux.at[s, 0:3, 0:back_rows], out_ux.at[s], in_ux.at[s]
         )
         if first:
             lax.fori_loop(0, K, pack_back, 0)
@@ -357,7 +365,8 @@
         if first:
             sty[s, C:W, :] = fold_low(roll(wm[4], 48))
         t_copies = to_column(
-            sty.at[s, 0:rows], lambda j: rty.at[s, j, 0:rows], out_ty.at[s], in_ty.at[s]
+            sty.at[s, 0:rows], lambda j: rty.at[s, j, 0:rows],
+            rty.at[s, 0:3, 0:rows], out_ty.at[s], in_ty.at[s]
         )
 
         arrived(u_copies)
@@ -389,7 +398,8 @@
         if first:
             suy[s, C:, :] = cur_map
         u_copies = to_column(
-            suy.at[s, 0:back_rows], lambda j: ruy.at[s, j, 0:back_rows], out_uy.at[s], in_uy.at[s]
+            suy.at[s, 0:back_rows], lambda j: ruy.at[s, j, 0:back_rows],
+            ruy.at[s, 0:3, 0:back_rows], out_uy.at[s], in_uy.at[s]
         )
         if first:
             for j in range(SIDE):
@@ -420,7 +430,7 @@
         for j in range(SIDE):
             into = r[W * j : W * (j + 1)]
             swz[s, j] = fold_low(into + w_own[j] if j else into)
-        t_copies = to_row(lambda j: swz.at[s, j], lambda j: rwz.at[s, j], out_wz.at[s], in_wz.at[s])
+        t_copies = to_row(lambda j: swz.at[s, j], lambda j: rwz.at[s, j], rwz.at[s, 0:3], out_wz.at[s], in_wz.at[s])
         r = mm(dp[1], entry)
         for j in range(SIDE):
             into = r[W * j : W * (j + 1)]
@@ -446,7 +456,7 @@
         r = mm(dp[2], rhs_of(pick[my_y]))
         for j in range(SIDE):
             syz[s, j] = fold_low(r[W * j : W * (j + 1)] + yloc[j])
-        u_copies = to_row(lambda j: syz.at[s, j], lambda j: ryz.at[s, j], out_yz.at[s], in_yz.at[s])
+        u_copies = to_row(lambda j: syz.at[s, j], lambda j: ryz.at[s, j], ryz.at[s, 0:3], out_yz.at[s], in_yz.at[s])
         if first:
             lax.fori_loop(K // 2, K, unfold_flux, 0)
 
@@ -470,47 +480,72 @@
         arrived(u_copies)
         arriving = rhs_of(assemble(ryz))
 
+        def last(m):
+            return mm(qh[1, 2 * W * m : 2 * W * (m + 1), :], arriving)
+
         low_copies, high_copies = [], []
+        following = last(0)
         for m in range(4):
-            r = mm(qh[1, 2 * W * m : 2 * W * (m + 1), :], arriving)
+            r, following = following, last(m + 1) if m < 3 else None
+            pieces = []
             for i in range(2):
                 k = 2 * m + i
                 y = yl[k] + r[W * i : W * (i + 1)]
                 yl[k] = y
                 upd[k] = RELAXATION * y if first else upd[k] + RELAXATION * y
-            low, high = edges(m)
+                pieces += [y[:, :L], y[:, L:]]
+            low, high = edges(pieces)
             sl[s, m] = low
             sh[s, m] = high
-            high_copies.append(send(sl.at[s, m], hh.at[s, m], send_l.at[s, m], recv_l.at[s, m], (before, line)))
-            low_copies.append(send(sh.at[s, m], hl.at[s, m], send_h.at[s, m], recv_h.at[s, m], (after, line)))
-
-        def inner(k, carry):
-            y = yl[k]
-            r = mm(fx[k], rhs_of(y))
-            parts = []
+            high_copies.append(send(sl.at[s, m], hh.at[s, m], send_l.at[s], recv_l.at[s, m], (before, line)))
+            low_copies.append(send(sh.at[s, m], hl.at[s, m], send_h.at[s], recv_h.at[s, m], (after, line)))
+        sent.append((sl.at[s], send_l.at[s]))
+        sent.append((sh.at[s], send_h.at[s]))
+
+        def inner(m, carry):
+            ys = [yl[2 * m + i] for i in range(2)]
+            rs = [mm(fx[2 * m + i], rhs_of(ys[i])) for i in range(2)]
+            for i in range(2):
+                k, y, r = 2 * m + i, ys[i], rs[i]
+                parts = []
+                for f in range(2):
+                    at = slice(L * f, L * (f + 1))
+                    acc = jnp.where(column > 0, roll(r[0:W, at], 1), 0.0)
+                    acc = acc + jnp.where(column < SX - 1, roll(r[W : 2 * W, at], -1), 0.0)
+                    acc = acc + jnp.where(lane >= SX, roll(r[2 * W : 3 * W, at], SX), 0.0)
+                    acc = acc + jnp.where(lane < L - SX, roll(r[3 * W :, at], -SX), 0.0)
+                    parts.append(acc)
+                turned = jnp.concatenate([-y[C:], y[:C]], axis=0)
+                acc = jnp.concatenate(parts, axis=1) + ph[pl.ds(k, 1), :] * turned
+                st[k] = KEEP * st[k] - RELAXATION * acc
+            return carry
+
+        lax.fori_loop(0, K // 2, inner, 0)
+
+        def put(out, k, x):
+            r = stored(jnp.concatenate([x[:, :L], x[:, L:]], axis=0))
             for f in range(2):
-                at = slice(L * f, L * (f + 1))
-                acc = jnp.where(column > 0, roll(r[0:W, at], 1), 0.0)
-                acc = acc + jnp.where(column < SX - 1, roll(r[W : 2 * W, at], -1), 0.0)
-                acc = acc + jnp.where(lane >= SX, roll(r[2 * W : 3 * W, at], SX), 0.0)
-                acc = acc + jnp.where(lane < L - SX, roll(r[3 * W :, at], -SX), 0.0)
-                parts.append(acc)
-            turned = jnp.concatenate([-y[C:], y[:C]], axis=0)
-            acc = jnp.concatenate(parts, axis=1) + ph[pl.ds(k, 1), :] * turned
-            st[k] = KEEP * st[k] - RELAXATION * acc
-            if not first:
-                for f in range(2):
-                    upd_out[k, pl.ds(f, W, stride=2), :] = stored(upd[k, :, L * f : L * (f + 1)])
-            return carry
-
-        lax.fori_loop(0, K, inner, 0)
-
-        for m in range(4):
+                out[k, pl.ds(f, W, stride=2), :] = r[W * f : W * (f + 1)]
+
+        if not first:
+
+            def put_update(k, carry):
+                put(upd_out, k, upd[k])
+                return carry
+
+            lax.fori_loop(0, K, put_update, 0, unroll=4)
+
+        def across(m):
             low_copies[m].wait_recv()
             high_copies[m].wait_recv()
             k0, k1 = 2 * m, 2 * m + 1
-            r_low = mm(jnp.concatenate([fx[k0, 2 * W : 3 * W, :], fx[k1, 2 * W : 3 * W, :]], axis=0), rhs_of(hl[s, m]))
-            r_high = mm(jnp.concatenate([fx[k0, 3 * W :, :], fx[k1, 3 * W :, :]], axis=0), rhs_of(hh[s, m]))
+            low = jnp.concatenate([fx[k0, 2 * W : 3 * W, :], fx[k1, 2 * W : 3 * W, :]], axis=0)
+            high = jnp.concatenate([fx[k0, 3 * W :, :], fx[k1, 3 * W :, :]], axis=0)
+            return mm(low, rhs_of(hl[s, m])), mm(high, rhs_of(hh[s, m]))
+
+        following = across(0)
+        for m in range(4):
+            (r_low, r_high), following = following, across(m + 1) if m < 3 else None
             for i in range(2):
                 k = 2 * m + i
                 parts = []
@@ -524,11 +559,10 @@
                     st[k] = current
                     x = step_down(k, x) if k else current
                 else:
-                    for f in range(2):
-                        res_out[k, pl.ds(f, W, stride=2), :] = stored(current[:, L * f : L * (f + 1)])
-
-    for copy in started:
-        copy.wait_send()
+                    put(res_out, k, current)
+
+    for ref, sem in sent:
+        bytes_of(ref, sem)
 
 
 def shards(residual, forward_maps, pivot_inverse, backward_maps, face_flux, mass_scale, frequencies, line_order):
@@ -578,8 +612,8 @@
             pltpu.VMEM((2, 4, W, L), F32),
             pltpu.VMEM((2, 4, W, L), F32),
             pltpu.VMEM((2, 4, W, L), F32),
-            *[dma((2, SIDE)) for _ in range(12)],
-            dma((2, 4)), dma((2, 4)), dma((2, 4)), dma((2, 4)),
+            *[dma((2,)) for _ in range(12)],
+            dma((2,)), dma((2, 4)), dma((2,)), dma((2, 4)),
         ],
         compiler_params=pltpu.CompilerParams(collective_id=0, has_side_effects=True),
         name="sweeps",

time: 57 us -> 55.3 us (0.970)
  Pallas kernels: 54.6 us -> 52.9 us
    pallas_call x1, Pallas kernels: 54.6 us -> 52.9 us  [shards(): pl.pallas_call(kernel, out_shape=(out, out), in_specs=[anywhere] * 8, out...]
where the time goes in v3:
time: 55.3 us; the launch traced here: 55.2 us
  Pallas kernels  52.9 us (96%)
  local copies, waits for them, and re-layouts  1.67 us (3%)
  between operations  0.64 us (1%)
    pallas_call x1, Pallas kernels, shards(): pl.pallas_call(kernel, out_shape=(out, out), in_specs=[anywhere] * 8, out...  52.9 us
    unnamed x2, local copies, waits for them, and re-layouts  1.67 us

profile of v3, /device:TPU:8, one launch (start us, length us, event | category | flops | bytes accessed | tf_op | source)
XLA Modules:
  0.0 55.2 jit_solution(12874761729395646557)
XLA Ops:
  0.6 52.9 %sweeps.1 = (f32[8,160,128]{2,1,0:T(8,128)S(1)}, f32[8,160,128]{2,1,0:T(8,128)S(1)}) custom-call(f32[8,160,128]{2,1,0:T(8,128)} %bitcast.6, f32[1,8,6400]{2,1,0:T(8,128)} %fwd_in.1, f32[1,8,6400]{2,1,0:T(8,128)} %piv_in.1, f32[1,8,6400]{2,1,0:T(8,128)} %bwd_in.1, f32[1,8,4,6400]{3,2,1,0:T(4,128)} %flux_in.1, f32[8,128]{1,0:T(8,128)} %mass_in.1, f32[2]{0:T(128)} %freq_in.1, ...), custom_call_target="tpu_custom_call" | custom-call | tf_op jit(solution)/shard_map/sweeps/pallas_call | solution.py:573
  53.5 0.8 %copy.12 = f32[8,80,2,128]{3,2,1,0:T(2,128)} copy(f32[8,80,2,128]{3,2,1,0:T(2,128)S(1)} %bitcast.5) | data formatting | bytes 1310720
  54.3 0.8 %copy.13 = f32[8,80,2,128]{3,2,1,0:T(2,128)} copy(f32[8,80,2,128]{3,2,1,0:T(2,128)S(1)} %bitcast.4) | data formatting | bytes 1310720

commit v4 on v3

--- a/solution.py
+++ b/solution.py
@@ -94,12 +94,12 @@
     res_in, fwd_in, piv_in, bwd_in, flux_in, mass_in, freq_in, order_in,
     upd_out, res_out,
     res, fwd, piv, bwd, flux, mass, freq, order, load_sem,
-    tops, xtops, fd, bn, fx, qh, rp, dp, cp,
+    placing, moved, spread, tops, xtops, fd, bn, fx, qh, rp, dp, cp,
     st, zz, yl, ym, upd, ph,
     stx, rtx, sux, rux, sty, rty, suy, ruy, swz, rwz, syz, ryz, yloc, cw, pick,
-    sl, sh, hl, hh,
+    sl, sh, hl, hh, hs, hn, nh, se, re,
     out_tx, in_tx, out_ux, in_ux, out_ty, in_ty, out_uy, in_uy,
-    out_wz, in_wz, out_yz, in_yz, send_l, recv_l, send_h, recv_h,
+    out_wz, in_wz, out_yz, in_yz, out_h, in_h, out_e, in_e, send_l, recv_l, send_h, recv_h,
 ):
     patch = lax.axis_index("patch")
     line = lax.axis_index("line")
@@ -156,6 +156,32 @@
 
     lane = lanes(W)
 
+    wide = lax.broadcasted_iota(jnp.int32, (1, 256), 1)
+    for i in range(2):
+        cell, slot = wide % L, 32 * (2 * i + wide // L)
+        for part, at in ((0, jnp.where(cell < SX, slot + cell, -1)), (1, jnp.where(cell >= L - SX, slot + cell - 96, -1))):
+            hit = jnp.where(lax.broadcasted_iota(jnp.int32, (L, 256), 0) == at, 1.0, 0.0).astype(BF16)
+            placing[0, i, 2 * L * part : 2 * L * part + L, :] = hit
+            placing[0, i, 2 * L * part + L : 2 * L * (part + 1), :] = hit
+
+    tall = lax.broadcasted_iota(jnp.int32, (L, L), 0)
+    for part, by in enumerate((-SX, SX)):
+        hit = jnp.where(tall == lanes(L) + by, 1.0, 0.0).astype(BF16)
+        moved[2 * L * part : 2 * L * part + L, :] = hit
+        moved[2 * L * part + L : 2 * L * (part + 1), :] = hit
+
+    wide = lax.broadcasted_iota(jnp.int32, (1, 512), 1)
+    place = wide % 256
+    group = place // W
+    value = place - W * group
+    swapped = jnp.where(value < C, value + C, value - C)
+    source = jnp.where(wide >= 256, swapped, value) + jnp.where(group == 2, L, 0)
+    source = jnp.where(group == 3, -1, source)
+    sign = jnp.where(wide >= 256, jnp.where(value < C, -1.0, 1.0), 1.0)
+    spread[...] = jnp.where(
+        lax.broadcasted_iota(jnp.int32, (256, 512), 0) == source, sign, 0.0
+    ).astype(BF16)
+
     def unfold_map(ref, which):
         def load(q):
             return ref[:, L * q : L * (q + 1)]
@@ -171,16 +197,16 @@
 
     place = lax.broadcasted_iota(jnp.int32, (L, L), 0)
     hot = jnp.where(order[...] == place, 1.0, 0.0).astype(BF16)
-    to_cells = jnp.concatenate([hot, hot], axis=1)
+    same = jnp.where(lanes(L) == place, 1.0, 0.0).astype(BF16)
+    turned_hot = lax.dot_general(same, hot, (((1,), (1,)), ((), ())), preferred_element_type=F32).astype(BF16)
+    to_cells = jnp.concatenate([turned_hot, turned_hot], axis=0)
     to_lines = jnp.concatenate([hot, hot], axis=0)
 
     def pair(x):
         return jnp.concatenate(two(x), axis=1)
 
     def grid(x):
-        return lax.dot_general(
-            pair(x), to_cells, (((1,), (1,)), ((), ())), preferred_element_type=F32
-        )
+        return mm(pair(x), to_cells)
 
     def stored(x):
         return mm(pair(x), to_lines)
@@ -192,20 +218,32 @@
         r = grid(jnp.concatenate([res[k, pl.ds(f, W, stride=2), :] for f in range(2)], axis=0))
         st[k] = jnp.concatenate([r[:W], r[W:]], axis=1)
 
-    def pack_down(k):
-        if k < K:
-            fd[k, 0:W, :] = lhs_of(top_of(0, k))
-            to_grid(k)
-        fd[k, W : 2 * W, :] = lhs_of(top_of(1, k - 1))
-        bn[k - 1] = lhs_of(-top_of(2, k - 1))
+    def packed(which, k0, count):
+        top = tops[which, k0 * C : (k0 + count) * C, :]
+        top = jnp.where(lanes(count * C) < W, top, 0.0)
+        r = mm(jnp.concatenate(two(top), axis=1), spread[...])
+        for k in range(count):
+            at = slice(C * k, C * (k + 1))
+            yield k0 + k, jnp.concatenate([r[at, :256], r[at, 256:]], axis=0)
+
+    def pack_down():
+        for k, block in packed(0, 0, K):
+            fd[k, 0:W, :] = block.astype(BF16)
+        for k, block in packed(1, 0, K):
+            fd[k + 1, W : 2 * W, :] = block.astype(BF16)
+
+    def pack_up():
+        for k, block in packed(2, 0, K):
+            bn[k] = (-block).astype(BF16)
 
     loads[2].wait()
     loads[3].wait()
     unfold_map(piv, 1)
     loads[4].wait()
     unfold_map(bwd, 2)
+    pack_down()
     to_grid(0)
-    pack_down(1)
+    to_grid(1)
 
     def unfold_flux(k, carry):
         def load(q):
@@ -224,6 +262,14 @@
         at = pl.ds(pl.multiple_of(k * W, W), W)
         qh[0, at, :] = lhs_of(real_form(tile, 80))
         qh[1, at, :] = lhs_of(real_form(tile, 40))
+        hs[k] = jnp.where(lanes(C) < W, tile[:C], roll(tile[C:], 48))
+        return carry
+
+    def pack_beside(k, carry):
+        at = pl.ds(pl.multiple_of(k * W, W), W)
+        for side in range(2):
+            part = hn[side, k]
+            nh[side, at, :] = lhs_of(real_form(jnp.concatenate([part, roll(part, -48)], axis=0), 40))
         return carry
 
     def step_down(k, x):
@@ -301,14 +347,18 @@
         return low, high
 
     column = lax.rem(lane, SX)
+    half = lane < 64
 
     for s in range(2):
         first = s == 0
         if first:
             x = jnp.concatenate([st[0], band(roll(top_of(0, 0), 80), 80, 120)], axis=1)
             for k in range(1, K):
-                pack_down(k + 1)
                 x = step_down(k, x)
+                if k + 1 < K:
+                    to_grid(k + 1)
+                if k == 3:
+                    pack_up()
             pl.semaphore_wait(barrier, 8)
         for f in range(2):
             t = x[:, L * f : L * (f + 1)]
@@ -339,11 +389,23 @@
         )
         if first:
             lax.fori_loop(0, K, pack_back, 0)
+            beside = [
+                send(hs, hn.at[0], out_h.at[0], in_h.at[0], (after, line)),
+                send(hs, hn.at[1], out_h.at[1], in_h.at[1], (before, line)),
+            ]
+            sent.append((hs, out_h.at[0]))
+            sent.append((hs, out_h.at[1]))
             loads[5].wait()
             loads[6].wait()
             cells_mass = grid(mass[...])
             for f in range(2):
                 ph[:, L * f : L * (f + 1)] = freq[f] * cells_mass
+
+        if not first:
+            for i in range(2):
+                for f in range(2):
+                    at = slice(L * f, L * (f + 1))
+                    placing[1, i, :, at] = mm(placing[0, i, :, at], to_lines[:L]).astype(BF16)
 
         arrived(t_copies)
         t = [unfold_low(rtx[s, j, 0:C, :]) for j in range(SIDE)]
@@ -408,6 +470,10 @@
             lax.fori_loop(0, SIDE, pack_row, 0)
             loads[7].wait()
             lax.fori_loop(0, K // 2, unfold_flux, 0)
+        else:
+            for copy in beside:
+                copy.wait_recv()
+            lax.fori_loop(0, K, pack_beside, 0)
         w_own, v_own = w, v
 
         arrived(t_copies)
@@ -473,32 +539,45 @@
 
         arrived(t_copies)
         incoming = rhs_of(assemble(rwz))
-        for m in range(4):
-            r = mm(qh[0, 2 * W * m : 2 * W * (m + 1), :], incoming)
-            for i in range(2):
-                yl[2 * m + i] = yl[2 * m + i] + r[W * i : W * (i + 1)]
-        arrived(u_copies)
-        arriving = rhs_of(assemble(ryz))
-
-        def last(m):
-            return mm(qh[1, 2 * W * m : 2 * W * (m + 1), :], arriving)
-
-        low_copies, high_copies = [], []
-        following = last(0)
-        for m in range(4):
-            r, following = following, last(m + 1) if m < 3 else None
-            pieces = []
+        def of_block(which, m, x):
+            return mm(qh[which, 2 * W * m : 2 * W * (m + 1), :], x)
+
+        low_copies, high_copies, e_copies = [], [], []
+
+        def add_block(which, m, r):
+            tiles = []
             for i in range(2):
                 k = 2 * m + i
                 y = yl[k] + r[W * i : W * (i + 1)]
                 yl[k] = y
-                upd[k] = RELAXATION * y if first else upd[k] + RELAXATION * y
-                pieces += [y[:, :L], y[:, L:]]
-            low, high = edges(pieces)
-            sl[s, m] = low
-            sh[s, m] = high
-            high_copies.append(send(sl.at[s, m], hh.at[s, m], send_l.at[s], recv_l.at[s, m], (before, line)))
-            low_copies.append(send(sh.at[s, m], hl.at[s, m], send_h.at[s], recv_h.at[s, m], (after, line)))
+                if which:
+                    upd[k] = RELAXATION * y if first else upd[k] + RELAXATION * y
+                tiles += [y[:, :L], y[:, L:]]
+            return tiles
+
+        def blocks(which, x, edges_too):
+            following = of_block(which, 0, x)
+            for m in range(4):
+                r, following = following, of_block(which, m + 1, x) if m < 3 else None
+                tiles = add_block(which, m, r)
+                if edges_too:
+                    sl[s, m], sh[s, m] = edges(tiles)
+                    high_copies.append(send(sl.at[s, m], hh.at[s, m], send_l.at[s], recv_l.at[s, m], (before, line)))
+                    low_copies.append(send(sh.at[s, m], hl.at[s, m], send_h.at[s], recv_h.at[s, m], (after, line)))
+
+        blocks(0, incoming, not first)
+        arrived(u_copies)
+        a = assemble(ryz)
+        if not first:
+            se[0] = fold_low(jnp.where(lane < SX, a[:, :L], roll(a[:, L:], SX)))
+            se[1] = fold_low(jnp.where(lane < SX, roll(a[:, :L], SX), roll(a[:, L:], 2 * SX)))
+            e_copies = [
+                send(se.at[1], re.at[0], out_e.at[1], in_e.at[0], (after, line)),
+                send(se.at[0], re.at[1], out_e.at[0], in_e.at[1], (before, line)),
+            ]
+            for side in range(2):
+                sent.append((se.at[side], out_e.at[side]))
+        blocks(1, rhs_of(a), first)
         sent.append((sl.at[s], send_l.at[s]))
         sent.append((sh.at[s], send_h.at[s]))
 
@@ -507,59 +586,82 @@
             rs = [mm(fx[2 * m + i], rhs_of(ys[i])) for i in range(2)]
             for i in range(2):
                 k, y, r = 2 * m + i, ys[i], rs[i]
+                rows = [
+                    jnp.concatenate([*two(r[2 * W : 3 * W, at]), *two(r[3 * W :, at])], axis=1)
+                    for at in (slice(0, L), slice(L, 2 * L))
+                ]
+                spanwise = mm(jnp.concatenate(rows, axis=0), moved[...])
                 parts = []
                 for f in range(2):
                     at = slice(L * f, L * (f + 1))
                     acc = jnp.where(column > 0, roll(r[0:W, at], 1), 0.0)
                     acc = acc + jnp.where(column < SX - 1, roll(r[W : 2 * W, at], -1), 0.0)
-                    acc = acc + jnp.where(lane >= SX, roll(r[2 * W : 3 * W, at], SX), 0.0)
-                    acc = acc + jnp.where(lane < L - SX, roll(r[3 * W :, at], -SX), 0.0)
-                    parts.append(acc)
+                    parts.append(acc + spanwise[W * f : W * (f + 1)])
                 turned = jnp.concatenate([-y[C:], y[:C]], axis=0)
                 acc = jnp.concatenate(parts, axis=1) + ph[pl.ds(k, 1), :] * turned
-                st[k] = KEEP * st[k] - RELAXATION * acc
+                new = KEEP * st[k] - RELAXATION * acc
+                if first:
+                    st[k] = new
+                else:
+                    put(k, upd[k], new)
             return carry
 
-        lax.fori_loop(0, K // 2, inner, 0)
-
-        def put(out, k, x):
-            r = stored(jnp.concatenate([x[:, :L], x[:, L:]], axis=0))
+        def put(k, a, b):
+            r = stored(jnp.concatenate([a[:, :L], a[:, L:], b[:, :L], b[:, L:]], axis=0))
             for f in range(2):
-                out[k, pl.ds(f, W, stride=2), :] = r[W * f : W * (f + 1)]
-
+                upd_out[k, pl.ds(f, W, stride=2), :] = r[W * f : W * (f + 1)]
+                res_out[k, pl.ds(f, W, stride=2), :] = r[W * (f + 2) : W * (f + 3)]
+
+        lax.fori_loop(0, 3 if first else 4, inner, 0)
+
+        extra = []
         if not first:
-
-            def put_update(k, carry):
-                put(upd_out, k, upd[k])
-                return carry
-
-            lax.fori_loop(0, K, put_update, 0, unroll=4)
+            for copy in (*low_copies, *high_copies, *e_copies):
+                copy.wait_recv()
+            for side in range(2):
+                e = unfold_low(re[side])
+                extra.append(mm(nh[side], rhs_of(jnp.where(half, e, roll(e, 64)))))
 
         def across(m):
-            low_copies[m].wait_recv()
-            high_copies[m].wait_recv()
             k0, k1 = 2 * m, 2 * m + 1
+            sides = [hl[s, m], hh[s, m]]
+            if extra:
+                sides = [
+                    a + jnp.where(half, x[W * k0 : W * k1], x[W * k1 : W * (k1 + 1)]) for a, x in zip(sides, extra)
+                ]
             low = jnp.concatenate([fx[k0, 2 * W : 3 * W, :], fx[k1, 2 * W : 3 * W, :]], axis=0)
             high = jnp.concatenate([fx[k0, 3 * W :, :], fx[k1, 3 * W :, :]], axis=0)
-            return mm(low, rhs_of(hl[s, m])), mm(high, rhs_of(hh[s, m]))
-
+            return mm(low, rhs_of(sides[0])), mm(high, rhs_of(sides[1]))
+
+        def placed(products, i):
+            at = slice(W * i, W * (i + 1))
+            edge = jnp.concatenate([*two(products[0][at]), *two(products[1][at])], axis=1)
+            return RELAXATION * mm(edge, placing[s, i])
+
+        def wait_for(m):
+            if first:
+                low_copies[m].wait_recv()
+                high_copies[m].wait_recv()
+
+        wait_for(0)
         following = across(0)
+        if first:
+            inner(3, 0)
         for m in range(4):
-            (r_low, r_high), following = following, across(m + 1) if m < 3 else None
+            products, following = following, None
+            if m < 3:
+                wait_for(m + 1)
+                following = across(m + 1)
             for i in range(2):
-                k = 2 * m + i
-                parts = []
-                for f in range(2):
-                    slot = 32 * (2 * i + f)
-                    low = roll(r_low[W * i : W * (i + 1)], -slot)
-                    high = roll(r_high[W * i : W * (i + 1)], 96 - slot)
-                    parts.append(jnp.where(lane < SX, low, jnp.where(lane >= L - SX, high, 0.0)))
-                current = st[k] - RELAXATION * jnp.concatenate(parts, axis=1)
+                k, part = 2 * m + i, placed(products, i)
                 if first:
+                    current = st[k] - part
                     st[k] = current
                     x = step_down(k, x) if k else current
                 else:
-                    put(res_out, k, current)
+                    for f in range(2):
+                        rows = pl.ds(f, W, stride=2)
+                        res_out[k, rows, :] = res_out[k, rows, :] - part[:, L * f : L * (f + 1)]
 
     for ref, sem in sent:
         bytes_of(ref, sem)
@@ -585,6 +687,9 @@
             pltpu.SMEM((2,), F32),
             pltpu.VMEM((1, L), jnp.int32),
             dma((8,)),
+            pltpu.VMEM((2, 2, 512, 256), BF16),
+            pltpu.VMEM((512, L), BF16),
+            pltpu.VMEM((256, 512), BF16),
             pltpu.VMEM((3, K * C, L), F32),
             pltpu.VMEM((4 * C, L), F32),
             pltpu.VMEM((K + 1, 2 * W, 256), BF16),
@@ -612,7 +717,11 @@
             pltpu.VMEM((2, 4, W, L), F32),
             pltpu.VMEM((2, 4, W, L), F32),
             pltpu.VMEM((2, 4, W, L), F32),
-            *[dma((2,)) for _ in range(12)],
+            pltpu.VMEM((K, C, L), F32), pltpu.VMEM((2, K, C, L), F32),
+            pltpu.VMEM((2, K * W, 256), BF16),
+            pltpu.VMEM((2, C, L), F32), pltpu.VMEM((2, C, L), F32),
+            *[dma((2,)) for _ in range(14)],
+            dma((2,)), dma((2,)),
             dma((2,)), dma((2, 4)), dma((2,)), dma((2, 4)),
         ],
         compiler_params=pltpu.CompilerParams(collective_id=0, has_side_effects=True),

time: 55.3 us -> 54.6 us (0.987)
  Pallas kernels: 52.9 us -> 52.2 us
    pallas_call x1, Pallas kernels: 52.9 us -> 52.2 us  [shards(): pl.pallas_call(kernel, out_shape=(out, out), in_specs=[anywhere] * 8, out...]
where the time goes in v4:
time: 54.6 us; the launch traced here: 54.5 us
  Pallas kernels  52.2 us (96%)
  local copies, waits for them, and re-layouts  1.67 us (3%)
  between operations  0.64 us (1%)
    pallas_call x1, Pallas kernels, shards(): pl.pallas_call(kernel, out_shape=(out, out), in_specs=[anywhere] * 8, out...  52.2 us
    unnamed x2, local copies, waits for them, and re-layouts  1.67 us

profile of v4, /device:TPU:8, one launch (start us, length us, event | category | flops | bytes accessed | tf_op | source)
XLA Modules:
  0.0 54.5 jit_solution(7267493474684079984)
XLA Ops:
  0.6 52.2 %sweeps.1 = (f32[8,160,128]{2,1,0:T(8,128)S(1)}, f32[8,160,128]{2,1,0:T(8,128)S(1)}) custom-call(f32[8,160,128]{2,1,0:T(8,128)} %bitcast.6, f32[1,8,6400]{2,1,0:T(8,128)} %fwd_in.1, f32[1,8,6400]{2,1,0:T(8,128)} %piv_in.1, f32[1,8,6400]{2,1,0:T(8,128)} %bwd_in.1, f32[1,8,4,6400]{3,2,1,0:T(4,128)} %flux_in.1, f32[8,128]{1,0:T(8,128)} %mass_in.1, f32[2]{0:T(128)} %freq_in.1, ...), custom_call_target="tpu_custom_call" | custom-call | tf_op jit(solution)/shard_map/sweeps/pallas_call | solution.py:675
  52.8 0.8 %copy.12 = f32[8,80,2,128]{3,2,1,0:T(2,128)} copy(f32[8,80,2,128]{3,2,1,0:T(2,128)S(1)} %bitcast.5) | data formatting | bytes 1310720
  53.6 0.8 %copy.13 = f32[8,80,2,128]{3,2,1,0:T(2,128)} copy(f32[8,80,2,128]{3,2,1,0:T(2,128)S(1)} %bitcast.4) | data formatting | bytes 1310720

commit v5 on v4

--- a/solution.py
+++ b/solution.py
@@ -612,7 +612,7 @@
                 upd_out[k, pl.ds(f, W, stride=2), :] = r[W * f : W * (f + 1)]
                 res_out[k, pl.ds(f, W, stride=2), :] = r[W * (f + 2) : W * (f + 3)]
 
-        lax.fori_loop(0, 3 if first else 4, inner, 0)
+        lax.fori_loop(0, 3, inner, 0)
 
         extra = []
         if not first:
@@ -645,8 +645,7 @@
 
         wait_for(0)
         following = across(0)
-        if first:
-            inner(3, 0)
+        inner(3, 0)
         for m in range(4):
             products, following = following, None
             if m < 3:

time: 54.6 us -> 54.9 us (level)
  the two profiles are of different devices: /device:TPU:8 before, /device:TPU:1 now
where the time goes in v5:
time: 54.9 us; the launch traced here: 54.8 us
  Pallas kernels  52.5 us (96%)
  local copies, waits for them, and re-layouts  1.67 us (3%)
  between operations  0.64 us (1%)
    pallas_call x1, Pallas kernels, shards(): pl.pallas_call(kernel, out_shape=(out, out), in_specs=[anywhere] * 8, out...  52.5 us
    unnamed x2, local copies, waits for them, and re-layouts  1.67 us

profile of v5, /device:TPU:1, one launch (start us, length us, event | category | flops | bytes accessed | tf_op | source)
XLA Modules:
  0.0 54.8 jit_solution(11458863723560351790)
XLA Ops:
  0.6 52.5 %sweeps.1 = (f32[8,160,128]{2,1,0:T(8,128)S(1)}, f32[8,160,128]{2,1,0:T(8,128)S(1)}) custom-call(f32[8,160,128]{2,1,0:T(8,128)} %bitcast.6, f32[1,8,6400]{2,1,0:T(8,128)} %fwd_in.1, f32[1,8,6400]{2,1,0:T(8,128)} %piv_in.1, f32[1,8,6400]{2,1,0:T(8,128)} %bwd_in.1, f32[1,8,4,6400]{3,2,1,0:T(4,128)} %flux_in.1, f32[8,128]{1,0:T(8,128)} %mass_in.1, f32[2]{0:T(128)} %freq_in.1, ...), custom_call_target="tpu_custom_call" | custom-call | tf_op jit(solution)/shard_map/sweeps/pallas_call | solution.py:674
  53.1 0.8 %copy.12 = f32[8,80,2,128]{3,2,1,0:T(2,128)} copy(f32[8,80,2,128]{3,2,1,0:T(2,128)S(1)} %bitcast.5) | data formatting | bytes 1310720
  53.9 0.8 %copy.13 = f32[8,80,2,128]{3,2,1,0:T(2,128)} copy(f32[8,80,2,128]{3,2,1,0:T(2,128)S(1)} %bitcast.4) | data formatting | bytes 1310720
